TPU v7x, 32 devices: a whole 2x2x4 slice. The times are simulated.
32 devices in a mesh: seq: 2 (over x), tensor: 4 (over y, core), dp: 4 (over z).
Axes of the slice: x: 2, y: 2, z: 4, core: 2. Of those that a mesh axis runs over, the one named last changes fastest.
Arguments:
- inputs: bfloat16 [4, 512, 3584], P('dp', 'seq'), may hold values from -6 to 6
- w_query: bfloat16 [3584, 2048], P(('seq', 'dp'), 'tensor'), may hold values from -0.09375 to 0.09375
- w_key: bfloat16 [3584, 1024], P(('seq', 'dp'), 'tensor'), may hold values from -0.09375 to 0.09375
- w_value: bfloat16 [3584, 1024], P(('seq', 'dp'), 'tensor'), may hold values from -0.09375 to 0.09375
- norm_gain: float32 [3584], replicated, may hold values from 0.1 to 1.9
- attn_grad: bfloat16 [4, 512, 2048], P('dp', 'seq', 'tensor'), may hold values from -200 to 200
Outputs:
- grad_query: float32 [3584, 2048], P(('seq', 'dp'), 'tensor')
- grad_key: float32 [3584, 1024], P(('seq', 'dp'), 'tensor')
- grad_value: float32 [3584, 1024], P(('seq', 'dp'), 'tensor')
- input_grad: bfloat16 [4, 512, 3584], P('dp', 'seq', 'tensor')
All inputs are finite; a program needn't handle non-finite values.
Results may differ from a plain program's by a relative error of at most 0.01.
Values may be sent and summed in bfloat16 or wider, within the bound.
A program may use at most 64 MiB of HBM per device.

v0:
```python
import math

import jax
import jax.numpy as jnp
from jax import lax
from jax.sharding import PartitionSpec as P

D = 3584
H = 8
KVH = 4
HD = 256
WINDOW = 256


EPSILON = 1e-06
SOFTCAP = 50.0
CLIP_BOUND = 1.0
ROPE_BASE = 10000.0


def shifted(value, axis, steps):
    count = lax.axis_size(axis)
    leading, last = (max(0, -steps), min(count, count - steps))
    return lax.ppermute(value, axis, [(source, source + steps) for source in range(leading, last)])


def angles(positions, head_width):
    frequency = ROPE_BASE ** (-2.0 * jnp.arange(head_width // 2).astype(jnp.float32) / head_width)
    phases = positions.astype(jnp.float32)[:, None] * frequency[None, :]
    return (jnp.cos(phases)[:, None, :], jnp.sin(phases)[:, None, :])


def rotate(vectors, cosine, sine_part, direction):
    half_width = vectors.shape[-1] // 2
    first_half = vectors[..., :half_width]
    second_half = vectors[..., half_width:]
    return jnp.concatenate(
        [
            first_half * cosine - direction * second_half * sine_part,
            second_half * cosine + direction * first_half * sine_part,
        ],
        -1,
    )


def attend(queries, key_rows, value_rows, query_pos, key_pos, cotangent):
    query_count, head_count, head_width = queries.shape
    kv_heads = key_rows.shape[1]
    group_size = head_count // kv_heads
    grouped_query = queries.reshape(query_count, kv_heads, group_size, head_width)
    grouped_cot = cotangent.reshape(query_count, kv_heads, group_size, head_width)
    inv_scale = 1.0 / math.sqrt(head_width)
    logits = (
        jnp.einsum("tkgd,skd->kgts", grouped_query, key_rows, preferred_element_type=jnp.float32)
        * inv_scale
    )
    squash = jnp.tanh(logits / SOFTCAP)
    allowed = (
        (key_pos[None, :] <= query_pos[:, None])
        & (key_pos[None, :] > query_pos[:, None] - WINDOW)
        & (key_pos[None, :] >= 0)
    )
    exp_terms = jnp.where(allowed, jnp.exp(SOFTCAP * squash), 0.0)
    softmax = exp_terms / jnp.sum(exp_terms, -1, keepdims=True)
    probs_low = softmax.astype(jnp.bfloat16)
    dsoftmax = jnp.einsum(
        "tkgd,skd->kgts", grouped_cot, value_rows, preferred_element_type=jnp.float32
    )
    value_grads = jnp.einsum(
        "kgts,tkgd->skd", probs_low, grouped_cot, preferred_element_type=jnp.float32
    )
    row_delta = jnp.sum(softmax * dsoftmax, -1, keepdims=True)
    dlogits = (softmax * (dsoftmax - row_delta) * (1.0 - squash * squash) * inv_scale).astype(
        jnp.bfloat16
    )
    dquery = jnp.einsum("kgts,skd->tkgd", dlogits, key_rows, preferred_element_type=jnp.float32)
    key_grads = jnp.einsum(
        "kgts,tkgd->skd", dlogits, grouped_query, preferred_element_type=jnp.float32
    )
    return (dquery.reshape(query_count, head_count, head_width), key_grads, value_grads)


def local(inputs, w_query, w_key, w_value, norm_gain, attn_grad):
    widened = inputs[0].astype(jnp.float32)
    row_count = widened.shape[0]
    inverse_rms = lax.rsqrt(jnp.mean(widened * widened, -1) + EPSILON)
    normed = (widened * inverse_rms[:, None] * norm_gain[None, :]).astype(jnp.bfloat16)
    width_q = w_query.shape[1]
    width_k = w_key.shape[1]
    local_w = jnp.concatenate([w_query, w_key, w_value], 1)
    full_w = lax.all_gather(local_w, ("seq", "dp"), axis=0, tiled=True)
    projected = jnp.dot(normed, full_w, preferred_element_type=jnp.float32)
    start_row = lax.axis_index("seq") * row_count
    query_pos = start_row + jnp.arange(row_count, dtype=jnp.int32)
    key_pos = start_row - row_count + jnp.arange(2 * row_count, dtype=jnp.int32)
    cosine, sine_part = angles(query_pos, HD)
    heads_q = width_q // HD
    heads_k = width_k // HD
    rotated_query = rotate(
        projected[:, :width_q].reshape(row_count, heads_q, HD), cosine, sine_part, 1.0
    ).astype(jnp.bfloat16)
    rotated_keys = rotate(
        projected[:, width_q : width_q + width_k].reshape(row_count, heads_k, HD),
        cosine,
        sine_part,
        1.0,
    ).astype(jnp.bfloat16)
    value_rows = (
        projected[:, width_q + width_k :].reshape(row_count, heads_k, HD).astype(jnp.bfloat16)
    )
    keys_before, values_before = shifted((rotated_keys, value_rows), "seq", 1)
    dquery, key_ext_grad, value_ext_grad = attend(
        rotated_query,
        jnp.concatenate([keys_before, rotated_keys], 0),
        jnp.concatenate([values_before, value_rows], 0),
        query_pos,
        key_pos,
        attn_grad[0],
    )
    back_keys, back_values = shifted(
        (key_ext_grad[:row_count], value_ext_grad[:row_count]), "seq", -1
    )
    key_grads = key_ext_grad[row_count:] + back_keys
    value_grads = value_ext_grad[row_count:] + back_values
    dquery = rotate(dquery, cosine, sine_part, -1.0)
    key_grads = rotate(key_grads, cosine, sine_part, -1.0)
    d_out = jnp.concatenate(
        [
            dquery.reshape(row_count, width_q),
            key_grads.reshape(row_count, width_k),
            value_grads.reshape(row_count, width_k),
        ],
        1,
    ).astype(jnp.bfloat16)
    columns = lax.all_to_all(normed, "seq", split_axis=1, concat_axis=0, tiled=True)
    grad_rows = lax.dot_general(
        columns,
        lax.all_gather(d_out, "seq", axis=0, tiled=True),
        (((0,), (0,)), ((), ())),
        preferred_element_type=jnp.float32,
    )
    square_sum = lax.psum(jnp.sum(grad_rows * grad_rows), ("seq", "tensor"))
    grad_rms = jnp.sqrt(square_sum / (D * (H + 2 * KVH) * HD) + EPSILON)
    factor = CLIP_BOUND / jnp.maximum(grad_rms, CLIP_BOUND)
    clipped = lax.psum_scatter(factor * grad_rows, "dp", scatter_dimension=0, tiled=True)
    dnormed = lax.dot_general(
        d_out, full_w, (((1,), (1,)), ((), ())), preferred_element_type=jnp.float32
    )
    part_width = D // lax.axis_size("tensor")
    offset = lax.axis_index("tensor") * part_width
    part_grad = lax.psum_scatter(dnormed, "tensor", scatter_dimension=1, tiled=True)
    gain_slab = lax.dynamic_slice_in_dim(norm_gain, offset, part_width, 0)
    input_slab = lax.dynamic_slice_in_dim(widened, offset, part_width, 1)
    scaled = gain_slab[None, :] * part_grad
    inner_sum = lax.psum(jnp.sum(input_slab * scaled, -1), "tensor")
    mean_term = (inner_sum / D)[:, None]
    input_grad = (
        inverse_rms[:, None] * scaled
        - input_slab * (inverse_rms * inverse_rms * inverse_rms)[:, None] * mean_term
    )
    return (
        clipped[:, :width_q],
        clipped[:, width_q : width_q + width_k],
        clipped[:, width_q + width_k :],
        input_grad.astype(jnp.bfloat16)[None],
    )


def solution(mesh):
    return jax.shard_map(
        local,
        mesh=mesh,
        in_specs=(
            P("dp", "seq", None),
            P(("seq", "dp"), "tensor"),
            P(("seq", "dp"), "tensor"),
            P(("seq", "dp"), "tensor"),
            P(),
            P("dp", "seq", "tensor"),
        ),
        out_specs=(
            P(("seq", "dp"), "tensor"),
            P(("seq", "dp"), "tensor"),
            P(("seq", "dp"), "tensor"),
            P("dp", "seq", "tensor"),
        ),
        check_vma=False,
    )
```

profile of v0, /device:TPU:0, one launch (start us, length us, event | category | flops | bytes accessed | tf_op | source)
XLA Modules:
  0.0 373.9 jit_solution(5908853757978191068)
XLA Ops:
  7.2 0.0 all-gather.3.cloned.1.call-start
  7.2 2.3 pad_maximum_fusion
  9.5 0.0 all-gather.3.cloned.1.call-update
  9.5 0.0 all-gather.5.cloned.1.call-start
  9.6 1.8 copy.62
  11.4 2.9 copy.35
  14.4 0.5 fusion
  14.9 0.6 multiply_multiply_fusion
  15.5 0.2 and_and_fusion
  15.7 1.2 broadcast_multiply_fusion.1
  16.9 108.0 %all-gather.3.cloned.1.call-done = bf16[3584,1024]{1,0:T(8,128)(2,1)} async-done(((bf16[448,1024]{1,0:T(8,128)(2,1)}), bf16[3584,1024]{1,0:T(8,128)(2,1)}) %all-gather.3.cloned.1.call-update) | async-done | bytes 7340048 | tf_op jit(solution)/shard_map/all_gather | solution.py:91
  124.9 5.3 %fusion.3 = f32[256,1024]{1,0:T(8,128)S(1)} fusion(bf16[3584,1024]{1,0:T(8,128)(2,1)} %all-gather.3.cloned.1.call-done, bf16[1,256,3584]{1,2,0:T(8,128)(2,1)S(1)} %copy.35, f32[3584]{0:T(1024)S(1)} %copy-done.9, f32[256]{0:T(256)S(1)} %get-tuple-element.20), kind=kOutput, calls=%fused_computation.8 | convolution fusion | flops 1882718208 | bytes 10238976 | tf_op jit(solution)/shard_map/dot_general | solution.py:92
  130.2 0.7 fusion.41
  130.9 3.1 collective-permute-start.1
  134.1 0.6 fusion.34
  134.6 0.3 reshape.263
  135.0 0.2 fusion.53
  135.2 1.3 collective-permute-start
  136.5 0.1 subtract_convert_fusion.1
  136.6 2.4 collective-permute-done
  139.0 0.5 fusion.16
  139.5 0.0 copy-start.4
  139.5 1.5 convolution_bitcast_fusion.2
  141.1 0.7 slice.87
  141.8 1.3 collective-permute-start.3
  143.1 1.4 multiply_reduce_fusion.1
  144.5 0.0 copy-start.1
  144.5 0.4 fusion.17
  145.0 0.3 convolution_bitcast_fusion.1
  145.3 0.7 slice.83
  146.0 1.3 collective-permute-start.2
  147.3 0.3 convolution_bitcast_fusion.3
  147.7 0.1 subtract_convert_fusion
  147.8 0.1 copy.43
  147.9 8.5 %collective-permute-done.2 = f32[256,1,256]{2,0,1:T(8,128)} collective-permute-done((f32[256,1,256]{2,0,1:T(8,128)}, f32[256,1,256]{2,0,1:T(8,128)}, u32[]{:S(2)}, u32[]{:S(2)}) %collective-permute-start.2) | collective-permute-done | bytes 262176 | tf_op jit(solution)/shard_map/ppermute | solution.py:24
  156.4 1.0 slice_add_fusion.1
  157.4 1.2 fusion.38
  158.7 0.1 copy.49
  158.8 1.0 fusion.42
  159.8 0.8 pad_maximum_fusion.1
  160.6 0.0 all-gather.5.cloned.1.call-update
  160.6 0.0 reduce-scatter.5.cloned.1.call-start
  160.7 7.0 %fusion.51 = f32[256,3584]{1,0:T(8,128)} fusion(bf16[3584,1024]{1,0:T(8,128)(2,1)} %all-gather.3.cloned.1.call-done, bf16[256,256]{0,1:T(8,128)(2,1)S(1)} %fusion.42, bf16[256,256]{0,1:T(8,128)(2,1)S(1)} %copy.49, bf16[256,512]{0,1:T(8,128)(2,1)S(1)} %bitcast.118), kind=kOutput, calls=%fused_computation.94 | convolution fusion | flops 1880621056 | bytes 11534336 | tf_op jit(solution)/shard_map/dot_general | solution.py:146
  167.7 0.0 reduce-scatter.5.cloned.1.call-update
  167.8 0.0 reduce-scatter.3.cloned.1.call-start
  167.8 0.3 convert_element_type.73
  168.1 0.3 copy-done.11
  168.4 0.6 multiply_convert_fusion
  169.1 31.4 %all_to_all.16 = bf16[256,2,1792]{0,2,1:T(8,128)(2,1)S(1)} all-to-all(bf16[256,2,1792]{0,2,1:T(8,128)(2,1)S(1)} %multiply_convert_fusion), channel_id=1, replica_groups=mesh['seq'=2,'tensor'=4,'dp'=4] {'seq'}, dimensions={1} | all-to-all | bytes 3670016 | tf_op jit(solution)/shard_map/all_to_all | solution.py:135
  200.5 2.4 copy.36
  202.9 7.7 %multiply_reduce_fusion = (f32[]{:T(128)}, f32[1792,1024]{1,0:T(8,128)}) fusion(bf16[512,1792]{1,0:T(8,128)(2,1)} %bitcast.116, bf16[512,1024]{0,1:T(8,128)(2,1)} %all-gather.5.cloned.1.call-done), kind=kOutput, calls=%fused_computation | convolution fusion | flops 1882718208 | bytes 10223620 | tf_op jit(solution)/shard_map/dot_general | solution.py:136
  210.6 13.5 %psum.14 = f32[]{:T(128)} all-reduce(f32[]{:T(128)} %get-tuple-element.25), channel_id=1, replica_groups=mesh['seq'=2,'tensor'=4,'dp'=4] {'seq','tensor'}, use_global_device_ids=true, to_apply=%region_4.5 | all-reduce | flops 1 | bytes 8 | tf_op jit(solution)/shard_map/psum | solution.py:142
  224.8 7.7 %broadcast_multiply_fusion = f32[1792,1024]{1,0:T(8,128)} fusion(f32[1792,1024]{1,0:T(8,128)} %get-tuple-element.26, f32[]{:T(128)S(6)} %div.41), kind=kLoop, calls=%fused_computation.6 | loop fusion | flops 1835008 | bytes 14680068 | tf_op jit(solution)/shard_map/mul | solution.py:145
  232.5 0.0 reduce-scatter.3.cloned.1.call-update
  232.5 0.1 dynamic_slice.8
  232.6 1.3 constant_dynamic-slice_fusion
  233.9 0.3 copy.50
  234.2 0.0 reduce-scatter.5.cloned.1.call-done
  234.2 1.4 fusion.14
  235.6 5.8 %psum.15 = f32[256]{0:T(256)S(1)} all-reduce(f32[256]{0:T(256)S(1)} %fusion.14), channel_id=1, replica_groups=mesh['seq'=2,'tensor'=4,'dp'=4] {'tensor'}, use_global_device_ids=true, to_apply=%region_8.9 | all-reduce | flops 256 | bytes 2048 | tf_op jit(solution)/shard_map/psum | solution.py:155
  241.4 2.4 fusion.21
  243.8 119.3 %reduce-scatter.3.cloned.1.call-done = f32[448,1024]{1,0:T(8,128)} async-done(((f32[1792,1024]{1,0:T(8,128)}), f32[448,1024]{1,0:T(8,128)}) %reduce-scatter.3.cloned.1.call-update) | async-done | bytes 1835024 | tf_op jit(solution)/shard_map/reduce_scatter | solution.py:145
  363.1 2.2 slice.88
  365.3 2.1 fusion.52
  (42 shorter events, 0.2 us)
Async XLA Ops:
  7.2 117.7 %all-gather.3.cloned.1.call-start = ((), (), s32[]{:S(2)}) async-start(), calls=%async_computation.3 | async-start | bytes 8257536 | tf_op jit(solution)/shard_map/all_gather | solution.py:91
  9.5 115.4 %copy-start.9 = (f32[3584]{0:T(1024)S(1)}, f32[3584]{0:T(1024)}, u32[]{:S(2)}) copy-start(f32[3584]{0:T(1024)} %param.10) | copy-start | bytes 43012
  9.5 193.4 %all-gather.5.cloned.1.call-start = ((), (), s32[]{:S(2)}) async-start(), calls=%async_computation.4 | async-start | bytes 1572864 | tf_op jit(solution)/shard_map/all_gather | solution.py:138
  14.3 119.8 %copy-start.13 = (f32[128]{0:T(128)}, f32[128]{0:T(128)S(1)}, u32[]{:S(2)}) copy-start(f32[128]{0:T(128)S(1)} %multiply_power_fusion) | copy-start | bytes 1540
  14.3 119.7 %copy-start.12 = (f32[256]{0:T(256)}, f32[256]{0:T(256)S(1)}, u32[]{:S(2)}) copy-start(f32[256]{0:T(256)S(1)} %fusion.44) | copy-start | bytes 3076
  15.5 114.7 %copy-start.10 = (f32[256]{0:T(256)}, f32[256]{0:T(256)S(1)}, u32[]{:S(2)}) copy-start(f32[256]{0:T(256)S(1)} %get-tuple-element.20) | copy-start | bytes 3076
  15.7 123.3 %copy-start.2 = (pred[256,512]{0,1:T(8,128)(4,1)}, pred[256,512]{0,1:T(8,128)(4,1)S(1)}, u32[]{:S(2)}) copy-start(pred[256,512]{0,1:T(8,128)(4,1)S(1)} %and_and_fusion) | copy-start | bytes 393220
  130.9 12.2 %collective-permute-start.1 = (bf16[256,1,256]{2,0,1:T(8,128)(2,1)}, bf16[256,1,256]{2,0,1:T(8,128)(2,1)}, u32[]{:S(2)}, u32[]{:S(2)}) collective-permute-start(bf16[256,1,256]{2,0,1:T(8,128)(2,1)} %fusion.41), channel_id=1, source_target_pairs={{0,16},{1,17},{2,18},{3,19},{4,20},{5,21},{6,22},{7,23},{8,24},{9,... | collective-permute-start | bytes 393224 | tf_op jit(solution)/shard_map/ppermute | solution.py:24
  134.6 4.9 %copy-start.5 = (bf16[256,1,128]{2,0,1:T(8,128)(2,1)}, bf16[256,1,128]{2,0,1:T(8,128)(2,1)S(1)}, u32[]{:S(2)}) copy-start(bf16[256,1,128]{2,0,1:T(8,128)(2,1)S(1)} %get-tuple-element.14) | copy-start | bytes 196612
  134.6 4.9 %copy-start.7 = (bf16[256,1,128]{2,0,1:T(8,128)(2,1)}, bf16[256,1,128]{2,0,1:T(8,128)(2,1)S(1)}, u32[]{:S(2)}) copy-start(bf16[256,1,128]{2,0,1:T(8,128)(2,1)S(1)} %get-tuple-element.15) | copy-start | bytes 196612
  135.2 3.8 %collective-permute-start = (bf16[256,1,256]{2,0,1:T(8,128)(2,1)S(1)}, bf16[256,1,256]{2,0,1:T(8,128)(2,1)S(1)}, u32[]{:S(2)}, u32[]{:S(2)}) collective-permute-start(bf16[256,1,256]{2,0,1:T(8,128)(2,1)S(1)} %pad_maximum_fusion.6), channel_id=1, source_target_pairs={{0,16},{1,17},{2,18},{3,19},{4,20},{5,21},{6,22},{7,23},{8,24},{9,... | collective-permute-start | bytes 393224 | tf_op jit(solution)/shard_map/ppermute | solution.py:24
  139.5 3.6 copy-start.3
  139.5 3.6 copy-start.4
  141.8 17.0 %collective-permute-start.3 = (f32[256,1,256]{0,2,1:T(8,128)}, f32[256,1,256]{0,2,1:T(8,128)}, u32[]{:S(2)}, u32[]{:S(2)}) collective-permute-start(f32[256,1,256]{0,2,1:T(8,128)} %slice.87), channel_id=1, source_target_pairs={{16,0},{17,1},{18,2},{19,3},{20,4},{21,5},{22,6},{23,7},{24,8},{25... | collective-permute-start | bytes 786440 | tf_op jit(solution)/shard_map/ppermute | solution.py:24
  144.5 2.8 copy-start.6
  144.5 2.8 copy-start.8
  144.5 3.2 copy-start.1
  146.0 10.4 %collective-permute-start.2 = (f32[256,1,256]{2,0,1:T(8,128)}, f32[256,1,256]{2,0,1:T(8,128)}, u32[]{:S(2)}, u32[]{:S(2)}) collective-permute-start(f32[256,1,256]{2,0,1:T(8,128)} %slice.83), channel_id=1, source_target_pairs={{16,0},{17,1},{18,2},{19,3},{20,4},{21,5},{22,6},{23,7},{24,8},{25... | collective-permute-start | bytes 786440 | tf_op jit(solution)/shard_map/ppermute | solution.py:24
  160.6 73.6 %reduce-scatter.5.cloned.1.call-start = ((), (), s32[]{:S(2)}) async-start(), calls=%async_computation.6 | async-start | bytes 4587520 | tf_op jit(solution)/shard_map/reduce_scatter | solution.py:151
  167.7 0.7 copy-start.11
  167.8 195.3 %reduce-scatter.3.cloned.1.call-start = ((), (), s32[]{:S(2)}) async-start(), calls=%async_computation.5 | async-start | bytes 9175040 | tf_op jit(solution)/shard_map/reduce_scatter | solution.py:145
  168.1 32.4 %copy-start = (f32[1,256,3584]{1,2,0:T(8,128)}, f32[1,256,3584]{1,2,0:T(8,128)S(1)}, u32[]{:S(2)}) copy-start(f32[1,256,3584]{1,2,0:T(8,128)S(1)} %convert_element_type.73) | copy-start | bytes 11010052
  232.5 8.8 %copy-start.14 = (f32[256]{0:T(256)S(1)}, f32[256]{0:T(256)}, u32[]{:S(2)}) copy-start(f32[256]{0:T(256)} %get-tuple-element.19) | copy-start | bytes 3076
Sparse Core Ops, SparseCore 0:
  10.7 114.1 all-gather.2
  160.8 27.5 all-gather.4
  190.9 42.1 reduce-scatter.4
  235.3 127.7 reduce-scatter.2
where the time goes:
time: 375 us; the launch traced here: 374 us
  waiting for transfers between devices  238 us (63%)
  blocking collectives  50.6 us (13%)
  matrix products  24 us (6%)
  other arithmetic  22.5 us (6%)
  local copies, waits for them, and re-layouts  16.4 us (4%)
  between operations  14.9 us (4%)
  starting transfers between devices  7.15 us (2%)
    reduce_scatter x1, waiting for transfers between devices, local(): lax.psum_scatter(factor * grad_rows, 'dp', scatter_dimension=0, tiled=True)  119 us
    all_gather x1, waiting for transfers between devices, local(): full_w = lax.all_gather(local_w, ('seq', 'dp'), axis=0, tiled=True)  108 us
    all_to_all x1, blocking collectives, local(): lax.all_to_all(normed, 'seq', split_axis=1, concat_axis=0, tiled=True)  31.4 us
    psum x1, blocking collectives, local(): square_sum = lax.psum(jnp.sum(grad_rows * grad_rows), ('seq', 'tensor'))  13.5 us
    ppermute x4, waiting for transfers between devices, shifted(): lax.ppermute(value, axis, [(source, source + steps) for source in range(l...  10.9 us
    dot_general x1, matrix products, local(): lax.dot_general(columns, lax.all_gather(d_out, 'seq', axis=0, tiled=True)...  7.73 us
    mul x1, other arithmetic, local(): factor * grad_rows  7.66 us
  transfers between devices with their start and end apart: 8, of which 4 were waited for; matrix products, arithmetic and copies ran while one was open for 13% of the time, Pallas kernels for 0%

commit v1 on v0

--- a/solution.py
+++ b/solution.py
@@ -1,8 +1,11 @@
+import functools
 import math
 
 import jax
 import jax.numpy as jnp
 from jax import lax
+from jax.experimental import pallas as pl
+from jax.experimental.pallas import tpu as pltpu
 from jax.sharding import PartitionSpec as P
 
 D = 3584
@@ -80,6 +83,216 @@
     return (dquery.reshape(query_count, head_count, head_width), key_grads, value_grads)
 
 
+MESH = pl.DeviceIdType.MESH
+
+
+def greet(axes):
+    barrier = pltpu.get_barrier_semaphore()
+    for axis in axes:
+        count = lax.axis_size(axis)
+        me = lax.axis_index(axis)
+        for step in (1, -1):
+
+            @pl.when((me + step >= 0) & (me + step < count))
+            def _():
+                pl.semaphore_signal(
+                    barrier, inc=1, device_id={axis: me + step}, device_id_type=MESH
+                )
+
+    near = 0
+    for axis in axes:
+        me = lax.axis_index(axis)
+        near = near + jnp.minimum(me, 1) + jnp.minimum(lax.axis_size(axis) - 1 - me, 1)
+    pl.semaphore_wait(barrier, near)
+
+
+class LineGather:
+    def __init__(self, order, part, first, second, low, high, x_ref, out_ref, send_sem, recv_sem):
+        self.order = order
+        self.part, self.first, self.second = part, first, second
+        self.rows = pl.ds(low, high - low)
+        self.x_ref, self.out_ref = x_ref, out_ref
+        self.send_sem, self.recv_sem = send_sem, recv_sem
+        self.me = {axis: lax.axis_index(axis) for axis in (first, second)}
+        self.count = {axis: lax.axis_size(axis) for axis in (first, second)}
+        self.sends = []
+
+    def slot(self, at):
+        return self.out_ref.at[tuple(at[axis] for axis in self.order) + (self.rows,)]
+
+    def copy(self, at, axis, step, own):
+        way = (0 if axis == "seq" else 2) + (0 if step == 1 else 1)
+        return pltpu.make_async_remote_copy(
+            src_ref=self.x_ref.at[self.rows] if own else self.slot(at),
+            dst_ref=self.slot(at),
+            send_sem=self.send_sem.at[self.part, way, at["seq"], at["dp"]],
+            recv_sem=self.recv_sem.at[self.part, at["seq"], at["dp"]],
+            device_id={axis: self.me[axis] + step},
+            device_id_type=MESH,
+        )
+
+    def inside(self, axis, value):
+        return (value >= 0) & (value < self.count[axis])
+
+    def send(self, at, axis, step, held, own=False):
+        ok = held & self.inside(axis, self.me[axis] + step)
+
+        @pl.when(ok)
+        def _():
+            self.copy(at, axis, step, own).start()
+
+        self.sends.append((at, axis, step, ok, own))
+
+    def receive(self, at, held):
+        @pl.when(held)
+        def _():
+            self.copy(at, self.first, 1, False).wait_recv()
+
+    def steps(self):
+        first, second = self.first, self.second
+        here = jnp.bool_(True)
+        for axis in (first, second):
+            for step in (1, -1):
+                self.send(dict(self.me), axis, step, here, True)
+        yield
+        column = [(dict(self.me), here, True)]
+        for hop in range(1, self.count[first]):
+            for step in (1, -1):
+                at = {**self.me, first: self.me[first] - step * hop}
+                held = self.inside(first, at[first])
+                self.receive(at, held)
+                self.send(at, first, step, held)
+                for way in (1, -1):
+                    self.send(at, second, way, held)
+                column.append((at, held, False))
+            yield
+        for hop in range(1, self.count[second]):
+            for base, held_base, _ in column:
+                for step in (1, -1):
+                    at = {**base, second: self.me[second] - step * hop}
+                    held = held_base & self.inside(second, at[second])
+                    self.receive(at, held)
+                    self.send(at, second, step, held)
+            yield
+
+    def finish(self):
+        for at, axis, step, ok, own in self.sends:
+
+            @pl.when(ok)
+            def _():
+                self.copy(at, axis, step, own).wait_send()
+
+
+def run_gathers(gathers):
+    live = [gather.steps() for gather in gathers]
+    while live:
+        still = []
+        for walk in live:
+            try:
+                next(walk)
+                still.append(walk)
+            except StopIteration:
+                pass
+        live = still
+    for gather in gathers:
+        gather.finish()
+
+
+def gather_kernel(cut, order, x_ref, out_ref, send_sem, recv_sem, own_sem):
+    rows = x_ref.shape[0]
+    own = pltpu.make_async_copy(
+        x_ref, out_ref.at[tuple(lax.axis_index(axis) for axis in order)], own_sem
+    )
+    own.start()
+    greet(("seq", "dp"))
+    run_gathers(
+        [
+            LineGather(order, 0, "seq", "dp", 0, cut, x_ref, out_ref, send_sem, recv_sem),
+            LineGather(order, 1, "dp", "seq", cut, rows, x_ref, out_ref, send_sem, recv_sem),
+        ]
+    )
+    own.wait()
+
+
+def gather_blocks(x, cut, order, collective_id):
+    shape = (lax.axis_size("seq"), lax.axis_size("dp"))
+    return pl.pallas_call(
+        functools.partial(gather_kernel, cut, order),
+        out_shape=jax.ShapeDtypeStruct(
+            tuple(lax.axis_size(axis) for axis in order) + x.shape, x.dtype
+        ),
+        in_specs=[pl.BlockSpec(memory_space=pltpu.VMEM)],
+        out_specs=pl.BlockSpec(memory_space=pl.ANY),
+        scratch_shapes=[
+            pltpu.SemaphoreType.DMA((2, 4) + shape),
+            pltpu.SemaphoreType.DMA((2,) + shape),
+            pltpu.SemaphoreType.DMA,
+        ],
+        compiler_params=pltpu.CompilerParams(
+            collective_id=collective_id, has_side_effects=True
+        ),
+    )(x)
+
+
+def exchange_kernel(x_ref, out_ref, send_sem, recv_sem, own_sem):
+    seqs, dps = lax.axis_size("seq"), lax.axis_size("dp")
+    seq, dp = lax.axis_index("seq"), lax.axis_index("dp")
+    barrier = pltpu.get_barrier_semaphore()
+    own = pltpu.make_async_copy(x_ref.at[seq, dp], out_ref.at[dp, seq], own_sem)
+    own.start()
+    peers = []
+    for ds in range(seqs):
+        for dd in range(dps):
+            if ds or dd:
+                peers.append((lax.rem(seq + ds, seqs), lax.rem(dp + dd, dps)))
+    for s, d in peers:
+        pl.semaphore_signal(
+            barrier, inc=1, device_id={"seq": s, "dp": d}, device_id_type=MESH
+        )
+    pl.semaphore_wait(barrier, len(peers))
+    for s, d in peers:
+        pltpu.make_async_remote_copy(
+            src_ref=x_ref.at[s, d],
+            dst_ref=out_ref.at[dp, seq],
+            send_sem=send_sem.at[s, d],
+            recv_sem=recv_sem.at[seq, dp],
+            device_id={"seq": s, "dp": d},
+            device_id_type=MESH,
+        ).start()
+    for s, d in peers:
+        pltpu.make_async_remote_copy(
+            src_ref=x_ref.at[s, d],
+            dst_ref=out_ref.at[d, s],
+            send_sem=send_sem.at[s, d],
+            recv_sem=recv_sem.at[s, d],
+            device_id={"seq": s, "dp": d},
+            device_id_type=MESH,
+        ).wait()
+    own.wait()
+
+
+def exchange_blocks(x, collective_id):
+    shape = x.shape[:2]
+    return pl.pallas_call(
+        exchange_kernel,
+        out_shape=jax.ShapeDtypeStruct((shape[1], shape[0]) + x.shape[2:], x.dtype),
+        in_specs=[pl.BlockSpec(memory_space=pltpu.VMEM)],
+        out_specs=pl.BlockSpec(memory_space=pl.ANY),
+        scratch_shapes=[
+            pltpu.SemaphoreType.DMA(shape),
+            pltpu.SemaphoreType.DMA(shape),
+            pltpu.SemaphoreType.DMA,
+        ],
+        compiler_params=pltpu.CompilerParams(
+            collective_id=collective_id, has_side_effects=True
+        ),
+    )(x)
+
+
+def cut_of(rows):
+    return max(16, rows // 7 // 16 * 16)
+
+
 def local(inputs, w_query, w_key, w_value, norm_gain, attn_grad):
     widened = inputs[0].astype(jnp.float32)
     row_count = widened.shape[0]
@@ -88,7 +301,10 @@
     width_q = w_query.shape[1]
     width_k = w_key.shape[1]
     local_w = jnp.concatenate([w_query, w_key, w_value], 1)
-    full_w = lax.all_gather(local_w, ("seq", "dp"), axis=0, tiled=True)
+    seqs, dps = lax.axis_size("seq"), lax.axis_size("dp")
+    rows_w = local_w.shape[0]
+    full_w = gather_blocks(local_w, cut_of(rows_w), ("seq", "dp"), 0).reshape(seqs * dps * rows_w, -1)
+    slabs = exchange_blocks(normed.T.reshape(seqs, dps, rows_w, row_count), 1)
     projected = jnp.dot(normed, full_w, preferred_element_type=jnp.float32)
     start_row = lax.axis_index("seq") * row_count
     query_pos = start_row + jnp.arange(row_count, dtype=jnp.int32)
@@ -132,17 +348,23 @@
         ],
         1,
     ).astype(jnp.bfloat16)
-    columns = lax.all_to_all(normed, "seq", split_axis=1, concat_axis=0, tiled=True)
-    grad_rows = lax.dot_general(
-        columns,
-        lax.all_gather(d_out, "seq", axis=0, tiled=True),
-        (((0,), (0,)), ((), ())),
-        preferred_element_type=jnp.float32,
-    )
-    square_sum = lax.psum(jnp.sum(grad_rows * grad_rows), ("seq", "tensor"))
+    cotangents = gather_blocks(d_out, cut_of(row_count), ("dp", "seq"), 2)
+    grads = []
+    for example in range(dps):
+        grads.append(
+            sum(
+                jnp.dot(
+                    slabs[example, s], cotangents[example, s], preferred_element_type=jnp.float32
+                )
+                for s in range(seqs)
+            )
+        )
+    square_sum = lax.psum(
+        jnp.stack([jnp.sum(grad * grad) for grad in grads]), ("seq", "tensor", "dp")
+    )
     grad_rms = jnp.sqrt(square_sum / (D * (H + 2 * KVH) * HD) + EPSILON)
     factor = CLIP_BOUND / jnp.maximum(grad_rms, CLIP_BOUND)
-    clipped = lax.psum_scatter(factor * grad_rows, "dp", scatter_dimension=0, tiled=True)
+    clipped = sum(factor[example] * grads[example] for example in range(dps))
     dnormed = lax.dot_general(
         d_out, full_w, (((1,), (1,)), ((), ())), preferred_element_type=jnp.float32
     )

time: 375 us -> 318 us (0.85)
  waiting for transfers between devices: 238 us -> 7.65 us
  Pallas kernels: 0 us -> 180 us
  local copies, waits for them, and re-layouts: 16.4 us -> 9.23 us
  blocking collectives: 50.6 us -> 43.5 us
  other arithmetic: 22.5 us -> 26.9 us
    pallas_call x0 -> x3, Pallas kernels: none -> 180 us  [the longest x2 141 us: gather_blocks(): pl.pallas_call(functools.partial(gather_kernel, cut, order), out_shape=ja...]
    reduce_scatter x1 -> x0, waiting for transfers between devices: 119 us -> none  [local(): lax.psum_scatter(factor * grad_rows, 'dp', scatter_dimension=0, tiled=True)]
    all_gather x2 -> x0, waiting for transfers between devices: 108 us -> none  [the longest x1 108 us: local(): full_w = lax.all_gather(local_w, ('seq', 'dp'), axis=0, tiled=True)]
    all_to_all x1 -> x0, blocking collectives: 31.4 us -> none  [local(): lax.all_to_all(normed, 'seq', split_axis=1, concat_axis=0, tiled=True)]
    psum x1, blocking collectives: 13.5 us -> 37.7 us  [local(): lax.psum(jnp.stack([jnp.sum(grad * grad) for grad in grads]), ('seq', 'te...]
    mul x1 -> x0, other arithmetic: 7.66 us -> none  [local(): factor * grad_rows]
    add x0 -> x1, other arithmetic: none -> 6.23 us  [local(): clipped = sum((factor[example] * grads[example] for example in range(dps)))]
    dot_general x1 -> x8, matrix products: 7.73 us -> 12.4 us  [local(): jnp.dot(slabs[example, s], cotangents[example, s], preferred_element_type...]
  transfers between devices with their start and end apart: 8 -> 5, of which waited for: 4 -> 2; matrix products, arithmetic and copies ran while one was open for 13% -> 13% of each run, Pallas kernels for 0% -> 29%
where the time goes in v1:
time: 318 us; the launch traced here: 317 us
  Pallas kernels  180 us (57%)
  blocking collectives  43.5 us (14%)
  other arithmetic  26.9 us (8%)
  matrix products  26.6 us (8%)
  between operations  14.5 us (5%)
  local copies, waits for them, and re-layouts  9.23 us (3%)
  starting transfers between devices  8.2 us (3%)
  waiting for transfers between devices  7.65 us (2%)
    pallas_call x2, Pallas kernels, gather_blocks(): pl.pallas_call(functools.partial(gather_kernel, cut, order), out_shape=ja...  141 us
    pallas_call x1, Pallas kernels, exchange_blocks(): pl.pallas_call(exchange_kernel, out_shape=jax.ShapeDtypeStruct((shape[1],...  39.1 us
    psum x1, blocking collectives, local(): lax.psum(jnp.stack([jnp.sum(grad * grad) for grad in grads]), ('seq', 'te...  37.7 us
    dot_general x8, matrix products, local(): jnp.dot(slabs[example, s], cotangents[example, s], preferred_element_type...  12.4 us
    ppermute x4, starting transfers between devices, shifted(): lax.ppermute(value, axis, [(source, source + steps) for source in range(l...  8.17 us
    ppermute x4, waiting for transfers between devices, shifted(): lax.ppermute(value, axis, [(source, source + steps) for source in range(l...  7.64 us
  transfers between devices with their start and end apart: 5, of which 2 were waited for; matrix products, arithmetic and copies ran while one was open for 13% of the time, Pallas kernels for 29%

profile of v1, /device:TPU:0, one launch (start us, length us, event | category | flops | bytes accessed | tf_op | source)
XLA Modules:
  0.0 316.9 jit_solution(3525882760431583794)
XLA Ops:
  7.2 0.0 reduce-scatter.2.cloned.1.call-start
  7.3 2.0 fusion
  9.3 0.6 multiply_multiply_fusion
  9.9 1.1 pad_maximum_fusion.x_ref
  11.0 86.9 %shard_map.94 = bf16[2,4,448,1024]{3,2,1,0:T(8,128)(2,1)} custom-call(bf16[448,1024]{1,0:T(8,128)(2,1)} %pad_maximum_fusion.x_ref), custom_call_target="tpu_custom_call" | custom-call | tf_op jit(solution)/shard_map/pallas_call | solution.py:219
  97.9 5.2 %fusion.4 = f32[256,1024]{1,0:T(8,128)S(1)} fusion(bf16[3584,1024]{1,0:T(8,128)(2,1)} %bitcast.192, bf16[1,256,3584]{2,1,0:T(8,128)(2,1)S(1)} %copy-done.1, f32[3584]{0:T(1024)S(1)} %copy-done.13, f32[256]{0:T(256)S(1)} %get-tuple-element.20), kind=kOutput, calls=%fused_computation.7 | convolution fusion | flops 1882718208 | bytes 10238976 | tf_op jit(solution)/shard_map/dot_general | solution.py:308
  103.1 0.6 fusion.71
  103.7 0.0 copy-start.7
  103.7 0.0 copy-start.9
  103.7 0.7 pad_maximum_fusion.5
  104.4 3.1 collective-permute-start
  107.5 0.7 fusion.78
  108.1 2.1 collective-permute-start.1
  110.2 0.5 broadcast_multiply_fusion
  110.8 0.5 iota_add_fusion.1
  111.3 0.6 iota_add_fusion
  111.9 0.5 broadcast_compare_fusion
  112.4 0.3 reshape.268
  112.8 0.2 fusion.90
  113.0 0.1 copy.37
  113.1 0.1 subtract_convert_fusion.1
  113.2 0.9 and_and_fusion
  114.1 1.5 fusion.17
  115.6 1.4 multiply_reduce_fusion.4
  116.9 0.0 copy-start.8
  117.0 0.4 fusion.18
  117.4 0.3 convolution_bitcast_fusion.1
  117.7 0.1 copy-done.8
  117.8 0.0 copy-done.10
  117.8 1.4 convolution_bitcast_fusion.3
  119.3 0.1 subtract_convert_fusion
  119.5 1.6 collective-permute-start.2
  121.0 0.4 convolution_bitcast_fusion.2
  121.5 1.5 collective-permute-start.3
  123.0 5.5 %collective-permute-done.2 = f32[256,1,256]{2,0,1:T(8,128)S(1)} collective-permute-done((f32[256,1,256]{2,0,1:T(8,128)S(1)}, f32[256,1,256]{2,0,1:T(8,128)S(1)}, u32[]{:S(2)}, u32[]{:S(2)}) %collective-permute-start.2) | collective-permute-done | bytes 262176 | tf_op jit(solution)/shard_map/ppermute | solution.py:27
  128.5 0.6 fusion.75
  129.1 2.1 collective-permute-done.3
  131.3 4.1 %fusion.88 = f32[256,3584]{1,0:T(8,128)} fusion(bf16[3584,1024]{1,0:T(8,128)(2,1)S(1)} %bitcast.195, bf16[256,256]{1,0:T(8,128)(2,1)S(1)} %fusion.79, bf16[256,256]{1,0:T(8,128)(2,1)S(1)} %maximum_bitcast_fusion.4, bf16[256,512]{1,0:T(8,128)(2,1)S(1)} %bitcast.196), kind=kOutput, calls=%fused_computation.139 | convolution fusion | flops 1880621056 | bytes 11534336 | tf_op jit(solution)/shard_map/dot_general | solution.py:368
  135.4 0.0 reduce-scatter.2.cloned.1.call-update
  135.4 2.2 convert_element_type.58
  137.6 1.8 fusion.6
  139.4 3.8 %copy.10 = bf16[3584,256]{1,0:T(8,128)(2,1)} copy(bf16[3584,256]{0,1:T(8,128)(2,1)} %fusion.6) | data formatting | bytes 3670016 | tf_op jit(solution)/shard_map/transpose | solution.py:307
  143.2 39.1 %shard_map.93 = bf16[4,2,448,256]{3,2,1,0:T(8,128)(2,1)} custom-call(bf16[2,4,448,256]{3,2,1,0:T(8,128)(2,1)} %bitcast.191), custom_call_target="tpu_custom_call" | custom-call | tf_op jit(solution)/shard_map/pallas_call | solution.py:276
  182.3 0.9 pad_maximum_fusion.1.x_ref
  183.2 54.2 %shard_map.95 = bf16[4,2,256,1024]{3,2,1,0:T(8,128)(2,1)} custom-call(bf16[256,1024]{1,0:T(8,128)(2,1)} %pad_maximum_fusion.1.x_ref), custom_call_target="tpu_custom_call" | custom-call | tf_op jit(solution)/shard_map/pallas_call | solution.py:219
  237.4 1.6 fusion.29
  239.0 1.4 fusion.26
  240.5 0.4 fusion.23
  240.9 0.4 fusion.20
  241.3 1.1 copy-done.3
  242.4 1.2 multiply_reduce_fusion.3
  243.6 2.5 multiply_reduce_fusion.2
  246.2 2.4 multiply_reduce_fusion.1
  248.6 2.4 multiply_reduce_fusion
  251.0 2.7 pad_maximum_fusion.6
  253.6 0.1 dynamic_slice.8
  253.7 37.7 %psum.14 = f32[4]{0:T(128)S(1)} all-reduce(f32[4]{0:T(128)S(1)} %pad_maximum_fusion.6), channel_id=1, replica_groups=mesh['seq'=2,'tensor'=4,'dp'=4] {'seq','tensor','dp'}, use_global_device_ids=true, to_apply=%region_7.8 | all-reduce | flops 4 | bytes 32 | tf_op jit(solution)/shard_map/psum | solution.py:362
  291.4 0.6 fusion.91
  292.0 6.2 %multiply_add_fusion = f32[448,1024]{1,0:T(8,128)S(1)} fusion(f32[448,1024]{1,0:T(8,128)} %get-tuple-element.30, f32[448,1024]{1,0:T(8,128)} %get-tuple-element.32, f32[448,1024]{1,0:T(8,128)} %get-tuple-element.34, f32[448,1024]{1,0:T(8,128)S(1)} %get-tuple-element.36, f32[]{:T(128)} %bitcast.62, f32[]{:T(128)} %bitcast.61, f32[]{:T(128)} %bitcast.60, ...), kind=kLoop, calls=%fused_computation.9 | loop fusion | flops 3211264 | bytes 9175056 | tf_op jit(solution)/shard_map/add | solution.py:367
  298.3 1.0 slice.168
  299.3 1.0 fusion.89
  300.3 1.7 fusion.15
  302.0 5.8 %psum.15 = f32[256]{0:T(256)S(1)} all-reduce(f32[256]{0:T(256)S(1)} %fusion.15), channel_id=1, replica_groups=mesh['seq'=2,'tensor'=4,'dp'=4] {'tensor'}, use_global_device_ids=true, to_apply=%region_10.11 | all-reduce | flops 256 | bytes 2048 | tf_op jit(solution)/shard_map/psum | solution.py:377
  307.8 2.2 fusion.42
  (57 shorter events, 0.4 us)
Async XLA Ops:
  7.2 2.8 copy-start.5
  7.2 2.8 copy-start.12
  7.2 2.8 copy-start.11
  7.2 293.1 %reduce-scatter.2.cloned.1.call-start = ((), (), s32[]{:S(2)}) async-start(), calls=%async_computation.1 | async-start | bytes 4587520 | tf_op jit(solution)/shard_map/reduce_scatter | solution.py:373
  7.3 102.9 %copy-start.18 = (f32[128]{0:T(128)}, f32[128]{0:T(128)S(1)}, u32[]{:S(2)}) copy-start(f32[128]{0:T(128)S(1)} %multiply_power_fusion) | copy-start | bytes 1540
  7.3 102.9 %copy-start.14 = (f32[256]{0:T(256)}, f32[256]{0:T(256)S(1)}, u32[]{:S(2)}) copy-start(f32[256]{0:T(256)S(1)} %fusion.81) | copy-start | bytes 3076
  9.9 87.9 %copy-start.16 = (f32[256]{0:T(256)}, f32[256]{0:T(256)S(1)}, u32[]{:S(2)}) copy-start(f32[256]{0:T(256)S(1)} %get-tuple-element.20) | copy-start | bytes 3076
  11.0 86.9 %copy-start.1 = (bf16[1,256,3584]{2,1,0:T(8,128)(2,1)S(1)}, bf16[1,256,3584]{2,1,0:T(8,128)(2,1)}, u32[]{:S(2)}) copy-start(bf16[1,256,3584]{2,1,0:T(8,128)(2,1)} %param.6) | copy-start | bytes 5505028
  11.0 86.9 %copy-start.13 = (f32[3584]{0:T(1024)S(1)}, f32[3584]{0:T(1024)}, u32[]{:S(2)}) copy-start(f32[3584]{0:T(1024)} %param.10) | copy-start | bytes 43012
  103.7 6.5 %copy-start.7 = (bf16[256,1,128]{2,0,1:T(8,128)(2,1)}, bf16[256,1,128]{2,0,1:T(8,128)(2,1)S(1)}, u32[]{:S(2)}) copy-start(bf16[256,1,128]{2,0,1:T(8,128)(2,1)S(1)} %get-tuple-element.14) | copy-start | bytes 196612
  103.7 6.5 %copy-start.9 = (bf16[256,1,128]{2,0,1:T(8,128)(2,1)}, bf16[256,1,128]{2,0,1:T(8,128)(2,1)S(1)}, u32[]{:S(2)}) copy-start(bf16[256,1,128]{2,0,1:T(8,128)(2,1)S(1)} %get-tuple-element.15) | copy-start | bytes 196612
  104.4 9.7 %collective-permute-start = (bf16[256,1,256]{2,0,1:T(8,128)(2,1)}, bf16[256,1,256]{2,0,1:T(8,128)(2,1)}, u32[]{:S(2)}, u32[]{:S(2)}) collective-permute-start(bf16[256,1,256]{2,0,1:T(8,128)(2,1)} %pad_maximum_fusion.5), channel_id=1, source_target_pairs={{0,16},{1,17},{2,18},{3,19},{4,20},{5,21},{6,22},{7,23},{8,24},{9,... | collective-permute-start | bytes 393224 | tf_op jit(solution)/shard_map/ppermute | solution.py:27
  108.1 4.8 %copy-start.6 = (bf16[1,256,512]{2,1,0:T(8,128)(2,1)S(1)}, bf16[1,256,512]{2,1,0:T(8,128)(2,1)}, u32[]{:S(2)}) copy-start(bf16[1,256,512]{2,1,0:T(8,128)(2,1)} %param.11) | copy-start | bytes 786436
  108.1 7.4 %collective-permute-start.1 = (bf16[256,1,256]{2,0,1:T(8,128)(2,1)}, bf16[256,1,256]{2,0,1:T(8,128)(2,1)}, u32[]{:S(2)}, u32[]{:S(2)}) collective-permute-start(bf16[256,1,256]{2,0,1:T(8,128)(2,1)} %fusion.78), channel_id=1, source_target_pairs={{0,16},{1,17},{2,18},{3,19},{4,20},{5,21},{6,22},{7,23},{8,24},{9,... | collective-permute-start | bytes 393224 | tf_op jit(solution)/shard_map/ppermute | solution.py:27
  116.9 0.8 copy-start.8
  116.9 0.9 copy-start.10
  117.4 13.9 %slice-start = ((s8[7340032]{0:T(1024)(128)(4,1)}), s8[4194304]{0:T(1024)(128)(4,1)S(1)}, s32[]{:S(2)}) async-start(s8[7340032]{0:T(1024)(128)(4,1)} %bitcast.193), calls=%async_computation.2 | async-start | bytes 8388608
  119.5 9.0 %copy-start.15 = (f32[256]{0:T(256)S(1)}, f32[256]{0:T(256)}, u32[]{:S(2)}) copy-start(f32[256]{0:T(256)} %copy-done.14) | copy-start | bytes 3076
  119.5 9.0 %copy-start.19 = (f32[128]{0:T(128)S(1)}, f32[128]{0:T(128)}, u32[]{:S(2)}) copy-start(f32[128]{0:T(128)} %copy-done.18) | copy-start | bytes 1540
  119.5 11.8 %slice-start.1 = ((s8[7340032]{0:T(1024)(128)(4,1)}), s8[3145728]{0:T(1024)(128)(4,1)S(1)}, s32[]{:S(2)}) async-start(s8[7340032]{0:T(1024)(128)(4,1)} %bitcast.193), calls=%async_computation.3 | async-start | bytes 6291456
  119.5 9.0 %collective-permute-start.2 = (f32[256,1,256]{2,0,1:T(8,128)S(1)}, f32[256,1,256]{2,0,1:T(8,128)S(1)}, u32[]{:S(2)}, u32[]{:S(2)}) collective-permute-start(f32[256,1,256]{2,0,1:T(8,128)S(1)} %slice.163), channel_id=1, source_target_pairs={{16,0},{17,1},{18,2},{19,3},{20,4},{21,5},{22,6},{23,7},{24,8},{25... | collective-permute-start | bytes 786440 | tf_op jit(solution)/shard_map/ppermute | solution.py:27
  121.5 9.8 %collective-permute-start.3 = (f32[256,1,256]{2,0,1:T(8,128)S(1)}, f32[256,1,256]{2,0,1:T(8,128)S(1)}, u32[]{:S(2)}, u32[]{:S(2)}) collective-permute-start(f32[256,1,256]{2,0,1:T(8,128)S(1)} %slice.167), channel_id=1, source_target_pairs={{16,0},{17,1},{18,2},{19,3},{20,4},{21,5},{22,6},{23,7},{24,8},{25... | collective-permute-start | bytes 786440 | tf_op jit(solution)/shard_map/ppermute | solution.py:27
  135.4 2.2 copy-start.17
  183.2 54.3 %copy-start.2 = (bf16[4,2,448,256]{3,2,1,0:T(8,128)(2,1)S(1)}, bf16[4,2,448,256]{3,2,1,0:T(8,128)(2,1)}, u32[]{:S(2)}) copy-start(bf16[4,2,448,256]{3,2,1,0:T(8,128)(2,1)} %shard_map.93) | copy-start | bytes 5505028
  237.4 3.1 copy-start
  240.9 1.5 copy-start.3
  299.3 8.5 %copy-start.20 = (f32[256]{0:T(256)S(1)}, f32[256]{0:T(256)}, u32[]{:S(2)}) copy-start(f32[256]{0:T(256)} %get-tuple-element.19) | copy-start | bytes 3076
  300.3 7.5 %copy-start.4 = (f32[256,896]{1,0:T(8,128)S(1)}, f32[256,896]{1,0:T(8,128)}, u32[]{:S(2)}) copy-start(f32[256,896]{1,0:T(8,128)} %reduce-scatter.2.cloned.1.call-done) | copy-start | bytes 2752516
Sparse Core Ops, SparseCore 0:
  135.5 42.1 reduce-scatter.1

commit v2 on v1

--- a/solution.py
+++ b/solution.py
@@ -86,7 +86,7 @@
 MESH = pl.DeviceIdType.MESH
 
 
-def greet(axes):
+def greet(axes, peers=()):
     barrier = pltpu.get_barrier_semaphore()
     for axis in axes:
         count = lax.axis_size(axis)
@@ -99,7 +99,9 @@
                     barrier, inc=1, device_id={axis: me + step}, device_id_type=MESH
                 )
 
-    near = 0
+    for peer in peers:
+        pl.semaphore_signal(barrier, inc=1, device_id=peer, device_id_type=MESH)
+    near = len(peers)
     for axis in axes:
         me = lax.axis_index(axis)
         near = near + jnp.minimum(me, 1) + jnp.minimum(lax.axis_size(axis) - 1 - me, 1)
@@ -232,6 +234,101 @@
             collective_id=collective_id, has_side_effects=True
         ),
     )(x)
+
+
+def tail_kernel(
+    cut,
+    order,
+    x_ref,
+    part_ref,
+    inner_ref,
+    out_ref,
+    parts_ref,
+    inners_ref,
+    send_sem,
+    recv_sem,
+    own_sem,
+    part_send,
+    part_recv,
+    inner_send,
+    inner_recv,
+):
+    rows = x_ref.shape[0]
+    count, me = lax.axis_size("tensor"), lax.axis_index("tensor")
+    width = part_ref.shape[1] // count
+
+    def slab(index):
+        return part_ref.at[:, pl.ds(pl.multiple_of(index * width, 128), width)]
+
+    owns = [
+        pltpu.make_async_copy(
+            x_ref, out_ref.at[tuple(lax.axis_index(axis) for axis in order)], own_sem.at[0]
+        ),
+        pltpu.make_async_copy(slab(me), parts_ref.at[me], own_sem.at[1]),
+        pltpu.make_async_copy(inner_ref, inners_ref.at[me], own_sem.at[2]),
+    ]
+    for own in owns:
+        own.start()
+    others = [lax.rem(me + hop, count) for hop in range(1, count)]
+    greet(("seq", "dp"), [{"tensor": other} for other in others])
+    copies = []
+    for index, other in enumerate(others):
+        copies.append(
+            pltpu.make_async_remote_copy(
+                src_ref=slab(other),
+                dst_ref=parts_ref.at[me],
+                send_sem=part_send.at[index],
+                recv_sem=part_recv.at[index],
+                device_id={"tensor": other},
+                device_id_type=MESH,
+            )
+        )
+        copies.append(
+            pltpu.make_async_remote_copy(
+                src_ref=inner_ref,
+                dst_ref=inners_ref.at[me],
+                send_sem=inner_send.at[index],
+                recv_sem=inner_recv.at[index],
+                device_id={"tensor": other},
+                device_id_type=MESH,
+            )
+        )
+    for copy in copies:
+        copy.start()
+    run_gathers(
+        [
+            LineGather(order, 0, "seq", "dp", 0, cut, x_ref, out_ref, send_sem, recv_sem),
+            LineGather(order, 1, "dp", "seq", cut, rows, x_ref, out_ref, send_sem, recv_sem),
+        ]
+    )
+    for copy in copies:
+        copy.wait()
+    for own in owns:
+        own.wait()
+
+
+def gather_and_scatter(x, part, inner, cut, order, collective_id):
+    shape = (lax.axis_size("seq"), lax.axis_size("dp"))
+    count = lax.axis_size("tensor")
+    return pl.pallas_call(
+        functools.partial(tail_kernel, cut, order),
+        out_shape=(
+            jax.ShapeDtypeStruct(tuple(lax.axis_size(axis) for axis in order) + x.shape, x.dtype),
+            jax.ShapeDtypeStruct((count, part.shape[0], part.shape[1] // count), part.dtype),
+            jax.ShapeDtypeStruct((count,) + inner.shape, inner.dtype),
+        ),
+        in_specs=[pl.BlockSpec(memory_space=pltpu.VMEM)] * 3,
+        out_specs=(pl.BlockSpec(memory_space=pl.ANY),) * 3,
+        scratch_shapes=[
+            pltpu.SemaphoreType.DMA((2, 4) + shape),
+            pltpu.SemaphoreType.DMA((2,) + shape),
+            pltpu.SemaphoreType.DMA((3,)),
+        ]
+        + [pltpu.SemaphoreType.DMA((count - 1,))] * 4,
+        compiler_params=pltpu.CompilerParams(
+            collective_id=collective_id, has_side_effects=True
+        ),
+    )(x, part, inner)
 
 
 def exchange_kernel(x_ref, out_ref, send_sem, recv_sem, own_sem):
@@ -348,7 +445,13 @@
         ],
         1,
     ).astype(jnp.bfloat16)
-    cotangents = gather_blocks(d_out, cut_of(row_count), ("dp", "seq"), 2)
+    dnormed = lax.dot_general(
+        d_out, full_w, (((1,), (1,)), ((), ())), preferred_element_type=jnp.float32
+    )
+    inner = jnp.sum(widened * norm_gain[None, :] * dnormed, -1).reshape(-1, 128)
+    cotangents, parts, inners = gather_and_scatter(
+        d_out, dnormed.astype(jnp.bfloat16), inner, cut_of(row_count), ("dp", "seq"), 2
+    )
     grads = []
     for example in range(dps):
         grads.append(
@@ -365,16 +468,13 @@
     grad_rms = jnp.sqrt(square_sum / (D * (H + 2 * KVH) * HD) + EPSILON)
     factor = CLIP_BOUND / jnp.maximum(grad_rms, CLIP_BOUND)
     clipped = sum(factor[example] * grads[example] for example in range(dps))
-    dnormed = lax.dot_general(
-        d_out, full_w, (((1,), (1,)), ((), ())), preferred_element_type=jnp.float32
-    )
     part_width = D // lax.axis_size("tensor")
     offset = lax.axis_index("tensor") * part_width
-    part_grad = lax.psum_scatter(dnormed, "tensor", scatter_dimension=1, tiled=True)
+    part_grad = jnp.sum(parts.astype(jnp.float32), 0)
     gain_slab = lax.dynamic_slice_in_dim(norm_gain, offset, part_width, 0)
     input_slab = lax.dynamic_slice_in_dim(widened, offset, part_width, 1)
     scaled = gain_slab[None, :] * part_grad
-    inner_sum = lax.psum(jnp.sum(input_slab * scaled, -1), "tensor")
+    inner_sum = jnp.sum(inners, 0).reshape(row_count)
     mean_term = (inner_sum / D)[:, None]
     input_grad = (
         inverse_rms[:, None] * scaled

time: 318 us -> 297 us (0.934)
  between operations: 14.5 us -> 1.14 us
  blocking collectives: 43.5 us -> 38.7 us
  other arithmetic: 26.9 us -> 22.4 us
    pallas_call x0 -> x1, Pallas kernels: none -> 54.4 us  [gather_and_scatter(): pl.pallas_call(functools.partial(tail_kernel, cut, order), out_shape=(jax...]
    pallas_call x2 -> x1, Pallas kernels: 141 us -> 86.9 us  [gather_blocks(): pl.pallas_call(functools.partial(gather_kernel, cut, order), out_shape=ja...]
    psum x1 -> x0, blocking collectives: 5.82 us -> none  [local(): inner_sum = lax.psum(jnp.sum(input_slab * scaled, -1), 'tensor')]
  transfers between devices with their start and end apart: 5 -> 4, of which waited for: 2 -> 2; matrix products, arithmetic and copies ran while one was open for 13% -> 3% of each run, Pallas kernels for 29% -> 0%
where the time goes in v2:
time: 297 us; the launch traced here: 296 us
  Pallas kernels  180 us (61%)
  blocking collectives  38.7 us (13%)
  matrix products  27.2 us (9%)
  other arithmetic  22.4 us (8%)
  local copies, waits for them, and re-layouts  10.7 us (4%)
  starting transfers between devices  8.03 us (3%)
  waiting for transfers between devices  7.61 us (3%)
    pallas_call x1, Pallas kernels, gather_blocks(): pl.pallas_call(functools.partial(gather_kernel, cut, order), out_shape=ja...  86.9 us
    pallas_call x1, Pallas kernels, gather_and_scatter(): pl.pallas_call(functools.partial(tail_kernel, cut, order), out_shape=(jax...  54.4 us
    pallas_call x1, Pallas kernels, exchange_blocks(): pl.pallas_call(exchange_kernel, out_shape=jax.ShapeDtypeStruct((shape[1],...  38.8 us
    psum x1, blocking collectives, local(): lax.psum(jnp.stack([jnp.sum(grad * grad) for grad in grads]), ('seq', 'te...  38.7 us
    dot_general x8, matrix products, local(): jnp.dot(slabs[example, s], cotangents[example, s], preferred_element_type...  12.3 us
    ppermute x4, starting transfers between devices, shifted(): lax.ppermute(value, axis, [(source, source + steps) for source in range(l...  8.03 us
    ppermute x4, waiting for transfers between devices, shifted(): lax.ppermute(value, axis, [(source, source + steps) for source in range(l...  7.61 us
    add x1, other arithmetic, local(): clipped = sum((factor[example] * grads[example] for example in range(dps)))  6.05 us
  transfers between devices with their start and end apart: 4, of which 2 were waited for; matrix products, arithmetic and copies ran while one was open for 3% of the time, Pallas kernels for 0%

profile of v2, /device:TPU:0, one launch (start us, length us, event | category | flops | bytes accessed | tf_op | source)
XLA Modules:
  0.0 295.9 jit_solution(12502353696219282947)
XLA Ops:
  0.7 2.0 fusion
  2.8 1.1 pad_maximum_fusion.x_ref
  3.8 86.9 %shard_map.94 = bf16[2,4,448,1024]{3,2,1,0:T(8,128)(2,1)} custom-call(bf16[448,1024]{1,0:T(8,128)(2,1)} %pad_maximum_fusion.x_ref), custom_call_target="tpu_custom_call" | custom-call | tf_op jit(solution)/shard_map/pallas_call | solution.py:221
  90.7 5.2 %fusion.6 = f32[256,1024]{1,0:T(8,128)S(1)} fusion(bf16[3584,1024]{1,0:T(8,128)(2,1)} %bitcast.197, bf16[1,256,3584]{2,1,0:T(8,128)(2,1)S(1)} %copy-done.2, f32[3584]{0:T(1024)S(1)} %copy-done.17, f32[256]{0:T(256)S(1)} %get-tuple-element.29), kind=kOutput, calls=%fused_computation.11 | convolution fusion | flops 1882718208 | bytes 10238976 | tf_op jit(solution)/shard_map/dot_general | solution.py:405
  95.9 0.6 fusion.72
  96.5 0.0 copy-start.10
  96.5 0.7 pad_maximum_fusion.5
  97.2 3.1 %collective-permute-start = (bf16[256,1,256]{2,0,1:T(8,128)(2,1)}, bf16[256,1,256]{2,0,1:T(8,128)(2,1)}, u32[]{:S(2)}, u32[]{:S(2)}) collective-permute-start(bf16[256,1,256]{2,0,1:T(8,128)(2,1)} %pad_maximum_fusion.5), channel_id=1, source_target_pairs={{0,16},{1,17},{2,18},{3,19},{4,20},{5,21},{6,22},{7,23},{8,24},{9,... | collective-permute-start | bytes 393224 | tf_op jit(solution)/shard_map/ppermute | solution.py:27
  100.3 0.7 fusion.79
  100.9 1.9 collective-permute-start.1
  102.9 0.5 broadcast_multiply_fusion
  103.5 0.6 iota_add_fusion.1
  104.0 0.5 broadcast_compare_fusion
  104.6 2.2 convert_element_type.64
  106.8 0.3 reshape.278
  107.1 0.2 fusion.91
  107.3 0.4 copy-done.6
  107.8 0.8 copy.37
  108.6 0.1 subtract_convert_fusion.1
  108.7 0.0 copy-start.7
  108.7 0.9 and_and_fusion
  109.6 0.0 collective-permute-done
  109.6 1.5 fusion.18
  111.1 0.0 collective-permute-done.1
  111.1 1.4 multiply_reduce_fusion.4
  112.5 0.0 copy-start.11
  112.5 0.4 fusion.19
  112.9 0.0 slice-start
  113.0 0.3 convolution_bitcast_fusion.1
  113.3 0.1 copy-done.9
  113.3 0.0 copy-done.11
  113.3 1.4 convolution_bitcast_fusion.3
  114.8 0.1 subtract_convert_fusion
  115.0 1.6 collective-permute-start.2
  116.5 0.4 convolution_bitcast_fusion.2
  117.0 0.0 copy-start.18
  117.0 1.5 collective-permute-start.3
  118.5 5.4 %collective-permute-done.2 = f32[256,1,256]{2,0,1:T(8,128)S(1)} collective-permute-done((f32[256,1,256]{2,0,1:T(8,128)S(1)}, f32[256,1,256]{2,0,1:T(8,128)S(1)}, u32[]{:S(2)}, u32[]{:S(2)}) %collective-permute-start.2) | collective-permute-done | bytes 262176 | tf_op jit(solution)/shard_map/ppermute | solution.py:27
  124.0 0.6 fusion.76
  124.6 2.2 collective-permute-done.3
  126.8 4.7 %fusion.4 = (f32[256]{0:T(256)}, bf16[256,3584]{1,0:T(8,128)(2,1)}, bf16[3584,256]{0,1:T(8,128)(2,1)}) fusion(bf16[1,256,3584]{2,1,0:T(8,128)(2,1)S(1)} %copy-done.2, f32[3584]{0:T(1024)S(1)} %copy-done.18, f32[256]{0:T(256)S(1)} %copy-done.15, bf16[3584,1024]{1,0:T(8,128)(2,1)S(1)} %bitcast.200, bf16[256,256]{1,0:T(8,128)(2,1)S(1)} %fusion.80, ...), kind=kOutput, calls=%fused_computation.7 | convolution fusion | flops 1887960832 | bytes 13385728 | tf_op jit(solution)/shard_map/dot_general | solution.py:448
  131.6 0.9 pad_maximum_fusion.1.x_ref
  132.4 3.8 %copy.10 = bf16[3584,256]{1,0:T(8,128)(2,1)} copy(bf16[3584,256]{0,1:T(8,128)(2,1)} %get-tuple-element.12) | data formatting | bytes 3670016 | tf_op jit(solution)/shard_map/transpose | solution.py:404
  136.2 38.8 %shard_map.93 = bf16[4,2,448,256]{3,2,1,0:T(8,128)(2,1)} custom-call(bf16[2,4,448,256]{3,2,1,0:T(8,128)(2,1)} %bitcast.196), custom_call_target="tpu_custom_call" | custom-call | tf_op jit(solution)/shard_map/pallas_call | solution.py:373
  175.1 54.4 %shard_map.95 = (bf16[4,2,256,1024]{3,2,1,0:T(8,128)(2,1)}, bf16[4,256,896]{2,1,0:T(8,128)(2,1)}, f32[4,2,128]{2,1,0:T(2,128)}) custom-call(bf16[256,1024]{1,0:T(8,128)(2,1)} %pad_maximum_fusion.1.x_ref, bf16[256,3584]{1,0:T(8,128)(2,1)} %get-tuple-element.11.part_ref, f32[2,128]{1,0:T(2,128)} %bitcast.205), custom_call_target="tpu_custom_call" | custom-call | tf_op jit(solution)/shard_map/pallas_call | solution.py:313
  229.5 1.6 fusion.30
  231.1 1.4 fusion.27
  232.5 0.4 fusion.24
  232.9 0.4 fusion.21
  233.3 1.1 copy-done.1
  234.4 1.2 multiply_reduce_fusion.3
  235.7 2.4 multiply_reduce_fusion.2
  238.0 2.5 multiply_reduce_fusion.1
  240.5 2.4 multiply_reduce_fusion
  242.9 2.7 pad_maximum_fusion.6
  245.6 0.1 dynamic_slice.8
  245.6 38.7 %psum.7 = f32[4]{0:T(128)S(1)} all-reduce(f32[4]{0:T(128)S(1)} %pad_maximum_fusion.6), channel_id=1, replica_groups=mesh['seq'=2,'tensor'=4,'dp'=4] {'seq','tensor','dp'}, use_global_device_ids=true, to_apply=%region_8.9 | all-reduce | flops 4 | bytes 32 | tf_op jit(solution)/shard_map/psum | solution.py:465
  284.4 0.6 fusion.92
  285.0 6.0 %multiply_add_fusion = f32[448,1024]{1,0:T(8,128)S(1)} fusion(f32[448,1024]{1,0:T(8,128)} %get-tuple-element.39, f32[448,1024]{1,0:T(8,128)} %get-tuple-element.41, f32[448,1024]{1,0:T(8,128)} %get-tuple-element.43, f32[448,1024]{1,0:T(8,128)S(1)} %get-tuple-element.45, f32[]{:T(128)} %bitcast.63, f32[]{:T(128)} %bitcast.62, f32[]{:T(128)} %bitcast.61, ...), kind=kLoop, calls=%fused_computation.13 | loop fusion | flops 3211264 | bytes 9175056 | tf_op jit(solution)/shard_map/add | solution.py:470
  291.1 1.0 fusion.90
  292.1 1.0 slice.168
  293.1 0.3 convert_reduce_fusion
  293.3 0.4 copy-done.16
  293.8 2.2 fusion.43
  (49 shorter events, 0.4 us)
Async XLA Ops:
  0.6 2.1 copy-start.5
  0.6 2.1 copy-start.13
  0.7 2.1 copy-start.12
  2.7 87.9 %copy-start.14 = (f32[256]{0:T(256)}, f32[256]{0:T(256)S(1)}, u32[]{:S(2)}) copy-start(f32[256]{0:T(256)S(1)} %get-tuple-element.29) | copy-start | bytes 3076
  3.8 86.9 %copy-start.2 = (bf16[1,256,3584]{2,1,0:T(8,128)(2,1)S(1)}, bf16[1,256,3584]{2,1,0:T(8,128)(2,1)}, u32[]{:S(2)}) copy-start(bf16[1,256,3584]{2,1,0:T(8,128)(2,1)} %param.6) | copy-start | bytes 5505028
  3.8 86.9 %copy-start.17 = (f32[3584]{0:T(1024)S(1)}, f32[3584]{0:T(1024)}, u32[]{:S(2)}) copy-start(f32[3584]{0:T(1024)} %param.10) | copy-start | bytes 43012
  96.5 6.4 %copy-start.8 = (bf16[256,1,128]{2,0,1:T(8,128)(2,1)}, bf16[256,1,128]{2,0,1:T(8,128)(2,1)S(1)}, u32[]{:S(2)}) copy-start(bf16[256,1,128]{2,0,1:T(8,128)(2,1)S(1)} %get-tuple-element.23) | copy-start | bytes 196612
  96.5 6.4 %copy-start.10 = (bf16[256,1,128]{2,0,1:T(8,128)(2,1)}, bf16[256,1,128]{2,0,1:T(8,128)(2,1)S(1)}, u32[]{:S(2)}) copy-start(bf16[256,1,128]{2,0,1:T(8,128)(2,1)S(1)} %get-tuple-element.24) | copy-start | bytes 196612
  97.2 12.4 %collective-permute-start = (bf16[256,1,256]{2,0,1:T(8,128)(2,1)}, bf16[256,1,256]{2,0,1:T(8,128)(2,1)}, u32[]{:S(2)}, u32[]{:S(2)}) collective-permute-start(bf16[256,1,256]{2,0,1:T(8,128)(2,1)} %pad_maximum_fusion.5), channel_id=1, source_target_pairs={{0,16},{1,17},{2,18},{3,19},{4,20},{5,21},{6,22},{7,23},{8,24},{9,... | collective-permute-start | bytes 393224 | tf_op jit(solution)/shard_map/ppermute | solution.py:27
  100.9 10.2 %collective-permute-start.1 = (bf16[256,1,256]{2,0,1:T(8,128)(2,1)}, bf16[256,1,256]{2,0,1:T(8,128)(2,1)}, u32[]{:S(2)}, u32[]{:S(2)}) collective-permute-start(bf16[256,1,256]{2,0,1:T(8,128)(2,1)} %fusion.79), channel_id=1, source_target_pairs={{0,16},{1,17},{2,18},{3,19},{4,20},{5,21},{6,22},{7,23},{8,24},{9,... | collective-permute-start | bytes 393224 | tf_op jit(solution)/shard_map/ppermute | solution.py:27
  106.8 0.9 copy-start.6
  108.7 2.4 copy-start.7
  112.5 0.8 copy-start.9
  112.5 0.9 copy-start.11
  112.9 13.8 %slice-start = ((s8[7340032]{0:T(1024)(128)(4,1)}), s8[4194304]{0:T(1024)(128)(4,1)S(1)}, s32[]{:S(2)}) async-start(s8[7340032]{0:T(1024)(128)(4,1)} %bitcast.198), calls=%async_computation | async-start | bytes 8388608
  115.0 11.8 %slice-start.1 = ((s8[7340032]{0:T(1024)(128)(4,1)}), s8[3145728]{0:T(1024)(128)(4,1)S(1)}, s32[]{:S(2)}) async-start(s8[7340032]{0:T(1024)(128)(4,1)} %bitcast.198), calls=%async_computation.1 | async-start | bytes 6291456
  115.0 8.9 %collective-permute-start.2 = (f32[256,1,256]{2,0,1:T(8,128)S(1)}, f32[256,1,256]{2,0,1:T(8,128)S(1)}, u32[]{:S(2)}, u32[]{:S(2)}) collective-permute-start(f32[256,1,256]{2,0,1:T(8,128)S(1)} %slice.163), channel_id=1, source_target_pairs={{16,0},{17,1},{18,2},{19,3},{20,4},{21,5},{22,6},{23,7},{24,8},{25... | collective-permute-start | bytes 786440 | tf_op jit(solution)/shard_map/ppermute | solution.py:27
  117.0 9.8 %copy-start.15 = (f32[256]{0:T(256)S(1)}, f32[256]{0:T(256)}, u32[]{:S(2)}) copy-start(f32[256]{0:T(256)} %copy-done.14) | copy-start | bytes 3076
  117.0 9.8 %copy-start.18 = (f32[3584]{0:T(1024)S(1)}, f32[3584]{0:T(1024)}, u32[]{:S(2)}) copy-start(f32[3584]{0:T(1024)} %param.10) | copy-start | bytes 43012
  117.0 9.7 %collective-permute-start.3 = (f32[256,1,256]{2,0,1:T(8,128)S(1)}, f32[256,1,256]{2,0,1:T(8,128)S(1)}, u32[]{:S(2)}, u32[]{:S(2)}) collective-permute-start(f32[256,1,256]{2,0,1:T(8,128)S(1)} %slice.167), channel_id=1, source_target_pairs={{16,0},{17,1},{18,2},{19,3},{20,4},{21,5},{22,6},{23,7},{24,8},{25... | collective-permute-start | bytes 786440 | tf_op jit(solution)/shard_map/ppermute | solution.py:27
  175.1 54.4 %copy-start = (bf16[4,2,448,256]{3,2,1,0:T(8,128)(2,1)S(1)}, bf16[4,2,448,256]{3,2,1,0:T(8,128)(2,1)}, u32[]{:S(2)}) copy-start(bf16[4,2,448,256]{3,2,1,0:T(8,128)(2,1)} %shard_map.93) | copy-start | bytes 5505028
  229.4 3.1 %copy-start.3 = (bf16[4,2,256,1024]{3,2,1,0:T(8,128)(2,1)S(1)}, bf16[4,2,256,1024]{3,2,1,0:T(8,128)(2,1)}, u32[]{:S(2)}) copy-start(bf16[4,2,256,1024]{3,2,1,0:T(8,128)(2,1)} %get-tuple-element.7) | copy-start | bytes 12582916
  232.9 1.5 copy-start.1
  291.0 2.0 copy-start.4
  293.1 0.7 copy-start.16

commit v3 on v2

--- a/solution.py
+++ b/solution.py
@@ -200,40 +200,55 @@
         gather.finish()
 
 
-def gather_kernel(cut, order, x_ref, out_ref, send_sem, recv_sem, own_sem):
+def head_kernel(
+    cut, x_ref, block_ref, out_ref, blocks_ref, send_sem, recv_sem, own_sem, *exchange_sems
+):
     rows = x_ref.shape[0]
-    own = pltpu.make_async_copy(
-        x_ref, out_ref.at[tuple(lax.axis_index(axis) for axis in order)], own_sem
-    )
-    own.start()
-    greet(("seq", "dp"))
+    seq, dp = lax.axis_index("seq"), lax.axis_index("dp")
+    owns = [
+        pltpu.make_async_copy(x_ref, out_ref.at[seq, dp], own_sem.at[0]),
+        pltpu.make_async_copy(block_ref.at[seq, dp], blocks_ref.at[dp, seq], own_sem.at[1]),
+    ]
+    for own in owns:
+        own.start()
+    _, peers = block_peers()
+    greet(
+        (),
+        [{"seq": seq, "dp": dp} for _, seq, dp in peers]
+        + [{"tensor": other} for other in tensor_peers()],
+    )
+    order = ("seq", "dp")
     run_gathers(
         [
             LineGather(order, 0, "seq", "dp", 0, cut, x_ref, out_ref, send_sem, recv_sem),
             LineGather(order, 1, "dp", "seq", cut, rows, x_ref, out_ref, send_sem, recv_sem),
+            Exchange(block_ref, blocks_ref, *exchange_sems),
         ]
     )
-    own.wait()
-
-
-def gather_blocks(x, cut, order, collective_id):
+    for own in owns:
+        own.wait()
+
+
+def gather_and_exchange(x, blocks, cut, collective_id):
     shape = (lax.axis_size("seq"), lax.axis_size("dp"))
     return pl.pallas_call(
-        functools.partial(gather_kernel, cut, order),
-        out_shape=jax.ShapeDtypeStruct(
-            tuple(lax.axis_size(axis) for axis in order) + x.shape, x.dtype
-        ),
-        in_specs=[pl.BlockSpec(memory_space=pltpu.VMEM)],
-        out_specs=pl.BlockSpec(memory_space=pl.ANY),
+        functools.partial(head_kernel, cut),
+        out_shape=(
+            jax.ShapeDtypeStruct(shape + x.shape, x.dtype),
+            jax.ShapeDtypeStruct((shape[1], shape[0]) + blocks.shape[2:], blocks.dtype),
+        ),
+        in_specs=[pl.BlockSpec(memory_space=pltpu.VMEM)] * 2,
+        out_specs=(pl.BlockSpec(memory_space=pl.ANY),) * 2,
         scratch_shapes=[
             pltpu.SemaphoreType.DMA((2, 4) + shape),
             pltpu.SemaphoreType.DMA((2,) + shape),
-            pltpu.SemaphoreType.DMA,
-        ],
+            pltpu.SemaphoreType.DMA((2,)),
+        ]
+        + exchange_semaphores(),
         compiler_params=pltpu.CompilerParams(
             collective_id=collective_id, has_side_effects=True
         ),
-    )(x)
+    )(x, blocks)
 
 
 def tail_kernel(
@@ -331,53 +346,169 @@
     )(x, part, inner)
 
 
-def exchange_kernel(x_ref, out_ref, send_sem, recv_sem, own_sem):
+def block_peers():
     seqs, dps = lax.axis_size("seq"), lax.axis_size("dp")
-    seq, dp = lax.axis_index("seq"), lax.axis_index("dp")
-    barrier = pltpu.get_barrier_semaphore()
-    own = pltpu.make_async_copy(x_ref.at[seq, dp], out_ref.at[dp, seq], own_sem)
+    mine = lax.axis_index("dp") * seqs + lax.axis_index("seq")
+    others = [lax.rem(mine + hop, seqs * dps) for hop in range(1, seqs * dps)]
+    return mine, [(other, lax.rem(other, seqs), other // seqs) for other in others]
+
+
+def tensor_peers():
+    count, me = lax.axis_size("tensor"), lax.axis_index("tensor")
+    return [lax.rem(me + hop, count) for hop in range(1, count)]
+
+
+class Exchange:
+    def __init__(self, x_ref, out_ref, send_sem, recv_sem, pass_sem):
+        self.x_ref, self.out_ref = x_ref, out_ref
+        self.send_sem, self.recv_sem, self.pass_sem = send_sem, recv_sem, pass_sem
+        self.seqs, self.dps = lax.axis_size("seq"), lax.axis_size("dp")
+        self.lanes, self.lane = lax.axis_size("tensor"), lax.axis_index("tensor")
+        self.mine, self.peers = block_peers()
+        self.sender = lax.rem(self.mine, self.lanes) == self.lane
+
+    def slot(self, index):
+        return self.out_ref.at[index // self.seqs, lax.rem(index, self.seqs)]
+
+    def first(self, hop):
+        _, seq, dp = self.peers[hop]
+        return pltpu.make_async_remote_copy(
+            src_ref=self.x_ref.at[seq, dp],
+            dst_ref=self.slot(self.mine),
+            send_sem=self.send_sem.at[hop],
+            recv_sem=self.recv_sem.at[self.mine],
+            device_id={"seq": seq, "dp": dp},
+            device_id_type=MESH,
+        )
+
+    def onward(self, index, step, hop, other):
+        return pltpu.make_async_remote_copy(
+            src_ref=self.slot(index),
+            dst_ref=self.slot(index),
+            send_sem=self.pass_sem.at[step, hop],
+            recv_sem=self.recv_sem.at[index],
+            device_id={"tensor": other},
+            device_id_type=MESH,
+        )
+
+    def owned(self, lane):
+        return [lane + step * self.lanes for step in range(self.seqs * self.dps // self.lanes)]
+
+    def steps(self):
+        @pl.when(self.sender)
+        def _():
+            for hop in range(len(self.peers)):
+                self.first(hop).start()
+
+        yield
+        others = tensor_peers()
+        for step, index in enumerate(self.owned(self.lane)):
+
+            @pl.when(index != self.mine)
+            def _():
+                self.onward(index, step, 0, others[0]).wait_recv()
+                for hop, other in enumerate(others):
+                    self.onward(index, step, hop, other).start()
+
+        yield
+
+    def finish(self):
+        others = tensor_peers()
+        for other in others:
+            for index in self.owned(other):
+
+                @pl.when(index != self.mine)
+                def _():
+                    self.onward(index, 0, 0, other).wait_recv()
+
+        for step, index in enumerate(self.owned(self.lane)):
+
+            @pl.when(index != self.mine)
+            def _():
+                for hop, other in enumerate(others):
+                    self.onward(index, step, hop, other).wait_send()
+
+        @pl.when(self.sender)
+        def _():
+            for hop in range(len(self.peers)):
+                self.first(hop).wait_send()
+
+
+def exchange_semaphores():
+    count, lanes = lax.axis_size("seq") * lax.axis_size("dp"), lax.axis_size("tensor")
+    return [
+        pltpu.SemaphoreType.DMA((count - 1,)),
+        pltpu.SemaphoreType.DMA((count,)),
+        pltpu.SemaphoreType.DMA((count // lanes, lanes - 1)),
+    ]
+
+
+def total_kernel(x_ref, out_ref, held, send_sem, recv_sem, send_wide, recv_wide, own_sem):
+    mine, peers = block_peers()
+    lane = lax.axis_index("tensor")
+    others = tensor_peers()
+    own = pltpu.make_async_copy(x_ref, held.at[lane, mine], own_sem)
     own.start()
-    peers = []
-    for ds in range(seqs):
-        for dd in range(dps):
-            if ds or dd:
-                peers.append((lax.rem(seq + ds, seqs), lax.rem(dp + dd, dps)))
-    for s, d in peers:
-        pl.semaphore_signal(
-            barrier, inc=1, device_id={"seq": s, "dp": d}, device_id_type=MESH
-        )
-    pl.semaphore_wait(barrier, len(peers))
-    for s, d in peers:
+    greet(
+        (),
+        [{"seq": seq, "dp": dp} for _, seq, dp in peers] + [{"tensor": other} for other in others],
+    )
+    near = [
         pltpu.make_async_remote_copy(
-            src_ref=x_ref.at[s, d],
-            dst_ref=out_ref.at[dp, seq],
-            send_sem=send_sem.at[s, d],
-            recv_sem=recv_sem.at[seq, dp],
-            device_id={"seq": s, "dp": d},
+            src_ref=x_ref,
+            dst_ref=held.at[lane, mine],
+            send_sem=send_sem.at[hop],
+            recv_sem=recv_sem.at[mine],
+            device_id={"seq": seq, "dp": dp},
             device_id_type=MESH,
-        ).start()
-    for s, d in peers:
+        )
+        for hop, (_, seq, dp) in enumerate(peers)
+    ]
+    for copy in near:
+        copy.start()
+    for index, seq, dp in peers:
         pltpu.make_async_remote_copy(
-            src_ref=x_ref.at[s, d],
-            dst_ref=out_ref.at[d, s],
-            send_sem=send_sem.at[s, d],
-            recv_sem=recv_sem.at[s, d],
-            device_id={"seq": s, "dp": d},
+            src_ref=x_ref,
+            dst_ref=held.at[lane, index],
+            send_sem=send_sem.at[0],
+            recv_sem=recv_sem.at[index],
+            device_id={"seq": seq, "dp": dp},
             device_id_type=MESH,
-        ).wait()
+        ).wait_recv()
     own.wait()
-
-
-def exchange_blocks(x, collective_id):
-    shape = x.shape[:2]
+    far = [
+        pltpu.make_async_remote_copy(
+            src_ref=held.at[lane],
+            dst_ref=held.at[lane],
+            send_sem=send_wide.at[hop],
+            recv_sem=recv_wide.at[hop],
+            device_id={"tensor": other},
+            device_id_type=MESH,
+        )
+        for hop, other in enumerate(others)
+    ]
+    for copy in far:
+        copy.start()
+    for copy in far:
+        copy.wait()
+    for copy in near:
+        copy.wait_send()
+    out_ref[...] = jnp.sum(held[...], (0, 1))
+
+
+def total_of(x, collective_id):
+    count, lanes = lax.axis_size("seq") * lax.axis_size("dp"), lax.axis_size("tensor")
     return pl.pallas_call(
-        exchange_kernel,
-        out_shape=jax.ShapeDtypeStruct((shape[1], shape[0]) + x.shape[2:], x.dtype),
+        total_kernel,
+        out_shape=jax.ShapeDtypeStruct(x.shape, x.dtype),
         in_specs=[pl.BlockSpec(memory_space=pltpu.VMEM)],
-        out_specs=pl.BlockSpec(memory_space=pl.ANY),
+        out_specs=pl.BlockSpec(memory_space=pltpu.VMEM),
         scratch_shapes=[
-            pltpu.SemaphoreType.DMA(shape),
-            pltpu.SemaphoreType.DMA(shape),
+            pltpu.VMEM((lanes, count) + x.shape, x.dtype),
+            pltpu.SemaphoreType.DMA((count - 1,)),
+            pltpu.SemaphoreType.DMA((count,)),
+            pltpu.SemaphoreType.DMA((lanes - 1,)),
+            pltpu.SemaphoreType.DMA((lanes - 1,)),
             pltpu.SemaphoreType.DMA,
         ],
         compiler_params=pltpu.CompilerParams(
@@ -400,8 +531,10 @@
     local_w = jnp.concatenate([w_query, w_key, w_value], 1)
     seqs, dps = lax.axis_size("seq"), lax.axis_size("dp")
     rows_w = local_w.shape[0]
-    full_w = gather_blocks(local_w, cut_of(rows_w), ("seq", "dp"), 0).reshape(seqs * dps * rows_w, -1)
-    slabs = exchange_blocks(normed.T.reshape(seqs, dps, rows_w, row_count), 1)
+    full_w, slabs = gather_and_exchange(
+        local_w, normed.T.reshape(seqs, dps, rows_w, row_count), cut_of(rows_w), 0
+    )
+    full_w = full_w.reshape(seqs * dps * rows_w, -1)
     projected = jnp.dot(normed, full_w, preferred_element_type=jnp.float32)
     start_row = lax.axis_index("seq") * row_count
     query_pos = start_row + jnp.arange(row_count, dtype=jnp.int32)
@@ -462,9 +595,8 @@
                 for s in range(seqs)
             )
         )
-    square_sum = lax.psum(
-        jnp.stack([jnp.sum(grad * grad) for grad in grads]), ("seq", "tensor", "dp")
-    )
+    squares = jnp.stack([jnp.sum(grad * grad) for grad in grads])
+    square_sum = total_of(jnp.broadcast_to(squares[:, None], (dps, 128)), 1)[:, 0]
     grad_rms = jnp.sqrt(square_sum / (D * (H + 2 * KVH) * HD) + EPSILON)
     factor = CLIP_BOUND / jnp.maximum(grad_rms, CLIP_BOUND)
     clipped = sum(factor[example] * grads[example] for example in range(dps))

time: 297 us -> 245 us (0.82)
  blocking collectives: 38.7 us -> 0 us
  Pallas kernels: 180 us -> 158 us
  other arithmetic: 22.4 us -> 26.7 us
    psum x1 -> x0, blocking collectives: 38.7 us -> none  [local(): lax.psum(jnp.stack([jnp.sum(grad * grad) for grad in grads]), ('seq', 'te...]
    pallas_call x2, Pallas kernels: 126 us -> 101 us  [the longest x1 89.7 us: gather_and_exchange(): pl.pallas_call(functools.partial(head_kernel, cut), out_shape=(jax.ShapeD...]
  transfers between devices with their start and end apart: 4 -> 4, of which waited for: 2 -> 2; matrix products, arithmetic and copies ran while one was open for 3% -> 4% of each run, Pallas kernels for 0% -> 0%
where the time goes in v3:
time: 245 us; the launch traced here: 244 us
  Pallas kernels  158 us (64%)
  other arithmetic  26.7 us (11%)
  matrix products  26.6 us (11%)
  local copies, waits for them, and re-layouts  11.4 us (5%)
  waiting for transfers between devices  10.4 us (4%)
  starting transfers between devices  10 us (4%)
    pallas_call x1, Pallas kernels, gather_and_exchange(): pl.pallas_call(functools.partial(head_kernel, cut), out_shape=(jax.ShapeD...  89.7 us
    pallas_call x1, Pallas kernels, gather_and_scatter(): pl.pallas_call(functools.partial(tail_kernel, cut, order), out_shape=(jax...  57 us
    dot_general x8, matrix products, local(): jnp.dot(slabs[example, s], cotangents[example, s], preferred_element_type...  12.3 us
    pallas_call x1, Pallas kernels, total_of(): pl.pallas_call(total_kernel, out_shape=jax.ShapeDtypeStruct(x.shape, x.dt...  11.2 us
    ppermute x4, waiting for transfers between devices, shifted(): lax.ppermute(value, axis, [(source, source + steps) for source in range(l...  10.4 us
    ppermute x4, starting transfers between devices, shifted(): lax.ppermute(value, axis, [(source, source + steps) for source in range(l...  10 us
    add x1, other arithmetic, local(): clipped = sum((factor[example] * grads[example] for example in range(dps)))  6.05 us
    dot_general x1, matrix products, local(): projected = jnp.dot(normed, full_w, preferred_element_type=jnp.float32)  5.18 us
  transfers between devices with their start and end apart: 4, of which 2 were waited for; matrix products, arithmetic and copies ran while one was open for 4% of the time, Pallas kernels for 0%

profile of v3, /device:TPU:0, one launch (start us, length us, event | category | flops | bytes accessed | tf_op | source)
XLA Modules:
  0.0 244.1 jit_solution(12039859136807835859)
XLA Ops:
  0.6 0.0 copy-start
  0.7 2.1 fusion
  2.7 0.6 multiply_multiply_fusion
  3.4 2.5 %fusion.8 = bf16[3584,256]{0,1:T(8,128)(2,1)} fusion(bf16[1,256,3584]{2,1,0:T(8,128)(2,1)S(1)} %copy-done, f32[3584]{0:T(1024)} %param.10, f32[256]{0:T(256)S(1)} %get-tuple-element.36), kind=kLoop, calls=%fused_computation.12 | loop fusion | flops 3670016 | bytes 3685376 | tf_op jit(solution)/shard_map/transpose | solution.py:535
  5.8 3.9 %copy.10 = bf16[3584,256]{1,0:T(8,128)(2,1)} copy(bf16[3584,256]{0,1:T(8,128)(2,1)} %fusion.8) | data formatting | bytes 3670016 | tf_op jit(solution)/shard_map/transpose | solution.py:535
  9.7 1.1 pad_maximum_fusion.x_ref
  10.8 89.7 %shard_map.93 = (bf16[2,4,448,1024]{3,2,1,0:T(8,128)(2,1)}, bf16[4,2,448,256]{3,2,1,0:T(8,128)(2,1)}) custom-call(bf16[448,1024]{1,0:T(8,128)(2,1)} %pad_maximum_fusion.x_ref, bf16[2,4,448,256]{3,2,1,0:T(8,128)(2,1)} %bitcast.196), custom_call_target="tpu_custom_call" | custom-call | tf_op jit(solution)/shard_map/pallas_call | solution.py:234
  100.5 5.2 %fusion.6 = f32[256,1024]{1,0:T(8,128)S(1)} fusion(bf16[3584,1024]{1,0:T(8,128)(2,1)} %bitcast.202, bf16[1,256,3584]{2,1,0:T(8,128)(2,1)S(1)} %copy-done, f32[3584]{0:T(1024)S(1)} %copy-done.14, f32[256]{0:T(256)S(1)} %get-tuple-element.36), kind=kOutput, calls=%fused_computation.11 | convolution fusion | flops 1882718208 | bytes 10238976 | tf_op jit(solution)/shard_map/dot_general | solution.py:538
  105.7 0.6 fusion.72
  106.3 0.0 copy-start.10
  106.3 0.7 pad_maximum_fusion.5
  107.0 5.1 %collective-permute-start = (bf16[256,1,256]{2,0,1:T(8,128)(2,1)}, bf16[256,1,256]{2,0,1:T(8,128)(2,1)}, u32[]{:S(2)}, u32[]{:S(2)}) collective-permute-start(bf16[256,1,256]{2,0,1:T(8,128)(2,1)} %pad_maximum_fusion.5), channel_id=1, source_target_pairs={{0,16},{1,17},{2,18},{3,19},{4,20},{5,21},{6,22},{7,23},{8,24},{9,... | collective-permute-start | bytes 393224 | tf_op jit(solution)/shard_map/ppermute | solution.py:27
  112.0 0.7 fusion.79
  112.7 1.9 collective-permute-start.1
  114.7 0.5 broadcast_multiply_fusion
  115.3 0.5 iota_add_fusion.1
  115.8 0.5 iota_add_fusion
  116.3 0.5 broadcast_compare_fusion
  116.9 2.2 convert_element_type.64
  119.1 0.3 reshape.286
  119.4 0.2 fusion.91
  119.6 0.4 copy-done.6
  120.0 0.8 copy.37
  120.9 0.1 dynamic_slice.8
  121.0 0.1 subtract_convert_fusion.1
  121.0 0.9 and_and_fusion
  121.9 1.5 fusion.18
  123.4 1.4 multiply_reduce_fusion.4
  124.8 0.0 copy-start.11
  124.8 0.4 fusion.19
  125.3 0.3 convolution_bitcast_fusion.1
  125.6 0.1 copy-done.9
  125.6 0.0 copy-done.11
  125.7 1.4 convolution_bitcast_fusion.3
  127.1 0.1 subtract_convert_fusion
  127.3 1.6 collective-permute-start.2
  128.9 0.4 convolution_bitcast_fusion.2
  129.3 1.5 collective-permute-start.3
  130.8 7.9 %collective-permute-done.2 = f32[256,1,256]{2,0,1:T(8,128)S(1)} collective-permute-done((f32[256,1,256]{2,0,1:T(8,128)S(1)}, f32[256,1,256]{2,0,1:T(8,128)S(1)}, u32[]{:S(2)}, u32[]{:S(2)}) %collective-permute-start.2) | collective-permute-done | bytes 262176 | tf_op jit(solution)/shard_map/ppermute | solution.py:27
  138.7 0.6 fusion.76
  139.3 2.5 %collective-permute-done.3 = f32[256,1,256]{2,0,1:T(8,128)S(1)} collective-permute-done((f32[256,1,256]{2,0,1:T(8,128)S(1)}, f32[256,1,256]{2,0,1:T(8,128)S(1)}, u32[]{:S(2)}, u32[]{:S(2)}) %collective-permute-start.3) | collective-permute-done | bytes 262176 | tf_op jit(solution)/shard_map/ppermute | solution.py:27
  141.9 4.1 %fusion.4 = (f32[256]{0:T(256)}, bf16[256,3584]{1,0:T(8,128)(2,1)}) fusion(bf16[1,256,3584]{2,1,0:T(8,128)(2,1)S(1)} %copy-done, f32[3584]{0:T(1024)S(1)} %copy-done.14, bf16[3584,1024]{1,0:T(8,128)(2,1)S(1)} %bitcast.205, bf16[256,256]{1,0:T(8,128)(2,1)S(1)} %fusion.80, bf16[256,256]{1,0:T(8,128)(2,1)S(1)} %maximum_bitcast_fusion.4, ...), kind=kOutput, calls=%fused_computation.7 | convolution fusion | flops 1885208320 | bytes 11549696 | tf_op jit(solution)/shard_map/dot_general | solution.py:581
  146.0 0.9 pad_maximum_fusion.1.x_ref
  146.9 57.0 %shard_map.94 = (bf16[4,2,256,1024]{3,2,1,0:T(8,128)(2,1)}, bf16[4,256,896]{2,1,0:T(8,128)(2,1)}, f32[4,2,128]{2,1,0:T(2,128)}) custom-call(bf16[256,1024]{1,0:T(8,128)(2,1)} %pad_maximum_fusion.1.x_ref, bf16[256,3584]{1,0:T(8,128)(2,1)} %get-tuple-element.15.part_ref, f32[2,128]{1,0:T(2,128)} %bitcast.201), custom_call_target="tpu_custom_call" | custom-call | tf_op jit(solution)/shard_map/pallas_call | solution.py:328
  203.9 1.6 fusion.30
  205.5 1.4 fusion.27
  207.0 0.4 fusion.24
  207.4 0.4 fusion.21
  207.8 1.1 copy-done.3
  208.9 1.2 multiply_reduce_fusion.3
  210.1 2.4 multiply_reduce_fusion.2
  212.5 2.5 %multiply_reduce_fusion.1 = (f32[]{:T(128)}, f32[448,1024]{1,0:T(8,128)}) fusion(f32[448,1024]{1,0:T(8,128)S(1)} %fusion.24, bf16[4,2,256,1024]{3,2,1,0:T(8,128)(2,1)S(1)} %copy-done.1, bf16[4,2,448,256]{3,2,1,0:T(8,128)(2,1)S(1)} %copy-done.3), kind=kOutput, calls=%fused_computation.15 | convolution fusion | flops 236257280 | bytes 4423684 | tf_op jit(solution)/shard_map/dot_general | solution.py:592
  214.9 2.4 multiply_reduce_fusion
  217.4 2.7 %pad_maximum_fusion.6 = f32[4]{0:T(128)S(1)} fusion(f32[1]{0:T(128)} %bitcast.59, f32[1]{0:T(128)} %bitcast.54, f32[1]{0:T(128)} %bitcast.49, f32[1]{0:T(128)} %bitcast.44), kind=kLoop, calls=%fused_computation.133 | loop fusion | flops 12 | bytes 32 | tf_op jit(solution)/shard_map/stack | solution.py:598
  220.0 0.7 broadcast_in_dim.12.x_ref
  220.7 11.2 %shard_map.95 = f32[4,128]{1,0:T(4,128)} custom-call(f32[4,128]{1,0:T(4,128)} %broadcast_in_dim.12.x_ref), custom_call_target="tpu_custom_call" | custom-call | tf_op jit(solution)/shard_map/pallas_call | solution.py:501
  231.9 0.7 maximum_divide_fusion
  232.6 0.5 fusion.92
  233.1 6.0 %multiply_add_fusion = f32[448,1024]{1,0:T(8,128)S(1)} fusion(f32[448,1024]{1,0:T(8,128)} %get-tuple-element.43, f32[448,1024]{1,0:T(8,128)} %get-tuple-element.45, f32[448,1024]{1,0:T(8,128)} %get-tuple-element.47, f32[448,1024]{1,0:T(8,128)S(1)} %get-tuple-element.49, f32[]{:T(128)} %bitcast.63, f32[]{:T(128)} %bitcast.62, f32[]{:T(128)} %bitcast.61, ...), kind=kLoop, calls=%fused_computation.13 | loop fusion | flops 3211264 | bytes 9175056 | tf_op jit(solution)/shard_map/add | solution.py:602
  239.2 1.0 fusion.90
  240.2 1.0 slice.176
  241.2 0.3 convert_reduce_fusion
  241.5 0.4 copy-done.22
  241.9 2.2 fusion.43
  (58 shorter events, 0.4 us)
Async XLA Ops:
  0.6 2.7 %copy-start = (bf16[1,256,3584]{2,1,0:T(8,128)(2,1)S(1)}, bf16[1,256,3584]{2,1,0:T(8,128)(2,1)}, u32[]{:S(2)}) copy-start(bf16[1,256,3584]{2,1,0:T(8,128)(2,1)} %param.6) | copy-start | bytes 5505028
  0.7 114.1 %copy-start.19 = (f32[128]{0:T(128)}, f32[128]{0:T(128)S(1)}, u32[]{:S(2)}) copy-start(f32[128]{0:T(128)S(1)} %multiply_power_fusion) | copy-start | bytes 1540
  3.3 97.1 %copy-start.17 = (f32[256]{0:T(256)}, f32[256]{0:T(256)S(1)}, u32[]{:S(2)}) copy-start(f32[256]{0:T(256)S(1)} %get-tuple-element.36) | copy-start | bytes 3076
  5.8 3.9 %copy-start.5 = (bf16[448,512]{1,0:T(8,128)(2,1)S(1)}, bf16[448,512]{1,0:T(8,128)(2,1)}, u32[]{:S(2)}) copy-start(bf16[448,512]{1,0:T(8,128)(2,1)} %param.7) | copy-start | bytes 1376260
  5.8 3.9 %copy-start.12 = (bf16[448,256]{1,0:T(8,128)(2,1)S(1)}, bf16[448,256]{1,0:T(8,128)(2,1)}, u32[]{:S(2)}) copy-start(bf16[448,256]{1,0:T(8,128)(2,1)} %param.9) | copy-start | bytes 688132
  5.8 3.9 %copy-start.13 = (bf16[448,256]{1,0:T(8,128)(2,1)S(1)}, bf16[448,256]{1,0:T(8,128)(2,1)}, u32[]{:S(2)}) copy-start(bf16[448,256]{1,0:T(8,128)(2,1)} %param.8) | copy-start | bytes 688132
  10.8 89.7 %copy-start.14 = (f32[3584]{0:T(1024)S(1)}, f32[3584]{0:T(1024)}, u32[]{:S(2)}) copy-start(f32[3584]{0:T(1024)} %param.10) | copy-start | bytes 43012
  105.7 11.2 %copy-start.15 = (f32[256]{0:T(256)}, f32[256]{0:T(256)S(1)}, u32[]{:S(2)}) copy-start(f32[256]{0:T(256)S(1)} %fusion.82) | copy-start | bytes 3076
  106.3 6.4 %copy-start.8 = (bf16[256,1,128]{2,0,1:T(8,128)(2,1)}, bf16[256,1,128]{2,0,1:T(8,128)(2,1)S(1)}, u32[]{:S(2)}) copy-start(bf16[256,1,128]{2,0,1:T(8,128)(2,1)S(1)} %get-tuple-element.26) | copy-start | bytes 196612
  106.3 6.4 %copy-start.10 = (bf16[256,1,128]{2,0,1:T(8,128)(2,1)}, bf16[256,1,128]{2,0,1:T(8,128)(2,1)S(1)}, u32[]{:S(2)}) copy-start(bf16[256,1,128]{2,0,1:T(8,128)(2,1)S(1)} %get-tuple-element.27) | copy-start | bytes 196612
  107.0 14.9 %collective-permute-start = (bf16[256,1,256]{2,0,1:T(8,128)(2,1)}, bf16[256,1,256]{2,0,1:T(8,128)(2,1)}, u32[]{:S(2)}, u32[]{:S(2)}) collective-permute-start(bf16[256,1,256]{2,0,1:T(8,128)(2,1)} %pad_maximum_fusion.5), channel_id=1, source_target_pairs={{0,16},{1,17},{2,18},{3,19},{4,20},{5,21},{6,22},{7,23},{8,24},{9,... | collective-permute-start | bytes 393224 | tf_op jit(solution)/shard_map/ppermute | solution.py:27
  112.7 10.7 %collective-permute-start.1 = (bf16[256,1,256]{2,0,1:T(8,128)(2,1)}, bf16[256,1,256]{2,0,1:T(8,128)(2,1)}, u32[]{:S(2)}, u32[]{:S(2)}) collective-permute-start(bf16[256,1,256]{2,0,1:T(8,128)(2,1)} %fusion.79), channel_id=1, source_target_pairs={{0,16},{1,17},{2,18},{3,19},{4,20},{5,21},{6,22},{7,23},{8,24},{9,... | collective-permute-start | bytes 393224 | tf_op jit(solution)/shard_map/ppermute | solution.py:27
  119.1 0.9 copy-start.6
  121.0 2.4 copy-start.7
  124.8 0.8 copy-start.9
  124.8 0.9 copy-start.11
  125.3 16.7 %slice-start = ((s8[7340032]{0:T(1024)(128)(4,1)}), s8[4194304]{0:T(1024)(128)(4,1)S(1)}, s32[]{:S(2)}) async-start(s8[7340032]{0:T(1024)(128)(4,1)} %bitcast.203), calls=%async_computation | async-start | bytes 8388608
  127.3 11.4 %copy-start.16 = (f32[256]{0:T(256)S(1)}, f32[256]{0:T(256)}, u32[]{:S(2)}) copy-start(f32[256]{0:T(256)} %copy-done.15) | copy-start | bytes 3076
  127.3 11.4 %copy-start.20 = (f32[128]{0:T(128)S(1)}, f32[128]{0:T(128)}, u32[]{:S(2)}) copy-start(f32[128]{0:T(128)} %copy-done.19) | copy-start | bytes 1540
  127.3 14.6 %slice-start.1 = ((s8[7340032]{0:T(1024)(128)(4,1)}), s8[3145728]{0:T(1024)(128)(4,1)S(1)}, s32[]{:S(2)}) async-start(s8[7340032]{0:T(1024)(128)(4,1)} %bitcast.203), calls=%async_computation.1 | async-start | bytes 6291456
  127.3 11.3 %collective-permute-start.2 = (f32[256,1,256]{2,0,1:T(8,128)S(1)}, f32[256,1,256]{2,0,1:T(8,128)S(1)}, u32[]{:S(2)}, u32[]{:S(2)}) collective-permute-start(f32[256,1,256]{2,0,1:T(8,128)S(1)} %slice.171), channel_id=1, source_target_pairs={{16,0},{17,1},{18,2},{19,3},{20,4},{21,5},{22,6},{23,7},{24,8},{25... | collective-permute-start | bytes 786440 | tf_op jit(solution)/shard_map/ppermute | solution.py:27
  129.3 12.5 %collective-permute-start.3 = (f32[256,1,256]{2,0,1:T(8,128)S(1)}, f32[256,1,256]{2,0,1:T(8,128)S(1)}, u32[]{:S(2)}, u32[]{:S(2)}) collective-permute-start(f32[256,1,256]{2,0,1:T(8,128)S(1)} %slice.175), channel_id=1, source_target_pairs={{16,0},{17,1},{18,2},{19,3},{20,4},{21,5},{22,6},{23,7},{24,8},{25... | collective-permute-start | bytes 786440 | tf_op jit(solution)/shard_map/ppermute | solution.py:27
  146.0 57.9 %copy-start.2 = (bf16[4,2,448,256]{3,2,1,0:T(8,128)(2,1)S(1)}, bf16[4,2,448,256]{3,2,1,0:T(8,128)(2,1)}, u32[]{:S(2)}) copy-start(bf16[4,2,448,256]{3,2,1,0:T(8,128)(2,1)} %get-tuple-element.9) | copy-start | bytes 5505028
  203.9 3.1 %copy-start.1 = (bf16[4,2,256,1024]{3,2,1,0:T(8,128)(2,1)S(1)}, bf16[4,2,256,1024]{3,2,1,0:T(8,128)(2,1)}, u32[]{:S(2)}) copy-start(bf16[4,2,256,1024]{3,2,1,0:T(8,128)(2,1)} %get-tuple-element.11) | copy-start | bytes 12582916
  207.4 1.5 copy-start.3
  239.2 2.0 copy-start.4
  241.2 0.7 copy-start.22
  241.2 0.7 copy-start.18
  241.2 0.7 copy-start.21

commit v4 on v3

--- a/solution.py
+++ b/solution.py
@@ -21,66 +21,10 @@
 ROPE_BASE = 10000.0
 
 
-def shifted(value, axis, steps):
-    count = lax.axis_size(axis)
-    leading, last = (max(0, -steps), min(count, count - steps))
-    return lax.ppermute(value, axis, [(source, source + steps) for source in range(leading, last)])
-
-
 def angles(positions, head_width):
     frequency = ROPE_BASE ** (-2.0 * jnp.arange(head_width // 2).astype(jnp.float32) / head_width)
     phases = positions.astype(jnp.float32)[:, None] * frequency[None, :]
     return (jnp.cos(phases)[:, None, :], jnp.sin(phases)[:, None, :])
-
-
-def rotate(vectors, cosine, sine_part, direction):
-    half_width = vectors.shape[-1] // 2
-    first_half = vectors[..., :half_width]
-    second_half = vectors[..., half_width:]
-    return jnp.concatenate(
-        [
-            first_half * cosine - direction * second_half * sine_part,
-            second_half * cosine + direction * first_half * sine_part,
-        ],
-        -1,
-    )
-
-
-def attend(queries, key_rows, value_rows, query_pos, key_pos, cotangent):
-    query_count, head_count, head_width = queries.shape
-    kv_heads = key_rows.shape[1]
-    group_size = head_count // kv_heads
-    grouped_query = queries.reshape(query_count, kv_heads, group_size, head_width)
-    grouped_cot = cotangent.reshape(query_count, kv_heads, group_size, head_width)
-    inv_scale = 1.0 / math.sqrt(head_width)
-    logits = (
-        jnp.einsum("tkgd,skd->kgts", grouped_query, key_rows, preferred_element_type=jnp.float32)
-        * inv_scale
-    )
-    squash = jnp.tanh(logits / SOFTCAP)
-    allowed = (
-        (key_pos[None, :] <= query_pos[:, None])
-        & (key_pos[None, :] > query_pos[:, None] - WINDOW)
-        & (key_pos[None, :] >= 0)
-    )
-    exp_terms = jnp.where(allowed, jnp.exp(SOFTCAP * squash), 0.0)
-    softmax = exp_terms / jnp.sum(exp_terms, -1, keepdims=True)
-    probs_low = softmax.astype(jnp.bfloat16)
-    dsoftmax = jnp.einsum(
-        "tkgd,skd->kgts", grouped_cot, value_rows, preferred_element_type=jnp.float32
-    )
-    value_grads = jnp.einsum(
-        "kgts,tkgd->skd", probs_low, grouped_cot, preferred_element_type=jnp.float32
-    )
-    row_delta = jnp.sum(softmax * dsoftmax, -1, keepdims=True)
-    dlogits = (softmax * (dsoftmax - row_delta) * (1.0 - squash * squash) * inv_scale).astype(
-        jnp.bfloat16
-    )
-    dquery = jnp.einsum("kgts,skd->tkgd", dlogits, key_rows, preferred_element_type=jnp.float32)
-    key_grads = jnp.einsum(
-        "kgts,tkgd->skd", dlogits, grouped_query, preferred_element_type=jnp.float32
-    )
-    return (dquery.reshape(query_count, head_count, head_width), key_grads, value_grads)
 
 
 MESH = pl.DeviceIdType.MESH
@@ -200,55 +144,40 @@
         gather.finish()
 
 
-def head_kernel(
-    cut, x_ref, block_ref, out_ref, blocks_ref, send_sem, recv_sem, own_sem, *exchange_sems
-):
+def gather_kernel(cut, order, x_ref, out_ref, send_sem, recv_sem, own_sem):
     rows = x_ref.shape[0]
-    seq, dp = lax.axis_index("seq"), lax.axis_index("dp")
-    owns = [
-        pltpu.make_async_copy(x_ref, out_ref.at[seq, dp], own_sem.at[0]),
-        pltpu.make_async_copy(block_ref.at[seq, dp], blocks_ref.at[dp, seq], own_sem.at[1]),
-    ]
-    for own in owns:
-        own.start()
-    _, peers = block_peers()
-    greet(
-        (),
-        [{"seq": seq, "dp": dp} for _, seq, dp in peers]
-        + [{"tensor": other} for other in tensor_peers()],
-    )
-    order = ("seq", "dp")
+    own = pltpu.make_async_copy(
+        x_ref, out_ref.at[tuple(lax.axis_index(axis) for axis in order)], own_sem
+    )
+    own.start()
+    greet(("seq", "dp"))
     run_gathers(
         [
             LineGather(order, 0, "seq", "dp", 0, cut, x_ref, out_ref, send_sem, recv_sem),
             LineGather(order, 1, "dp", "seq", cut, rows, x_ref, out_ref, send_sem, recv_sem),
-            Exchange(block_ref, blocks_ref, *exchange_sems),
         ]
     )
-    for own in owns:
-        own.wait()
-
-
-def gather_and_exchange(x, blocks, cut, collective_id):
+    own.wait()
+
+
+def gather_blocks(x, cut, order, collective_id):
     shape = (lax.axis_size("seq"), lax.axis_size("dp"))
     return pl.pallas_call(
-        functools.partial(head_kernel, cut),
-        out_shape=(
-            jax.ShapeDtypeStruct(shape + x.shape, x.dtype),
-            jax.ShapeDtypeStruct((shape[1], shape[0]) + blocks.shape[2:], blocks.dtype),
-        ),
-        in_specs=[pl.BlockSpec(memory_space=pltpu.VMEM)] * 2,
-        out_specs=(pl.BlockSpec(memory_space=pl.ANY),) * 2,
+        functools.partial(gather_kernel, cut, order),
+        out_shape=jax.ShapeDtypeStruct(
+            tuple(lax.axis_size(axis) for axis in order) + x.shape, x.dtype
+        ),
+        in_specs=[pl.BlockSpec(memory_space=pltpu.VMEM)],
+        out_specs=pl.BlockSpec(memory_space=pl.ANY),
         scratch_shapes=[
             pltpu.SemaphoreType.DMA((2, 4) + shape),
             pltpu.SemaphoreType.DMA((2,) + shape),
-            pltpu.SemaphoreType.DMA((2,)),
-        ]
-        + exchange_semaphores(),
+            pltpu.SemaphoreType.DMA,
+        ],
         compiler_params=pltpu.CompilerParams(
             collective_id=collective_id, has_side_effects=True
         ),
-    )(x, blocks)
+    )(x)
 
 
 def tail_kernel(
@@ -441,6 +370,209 @@
         pltpu.SemaphoreType.DMA((count,)),
         pltpu.SemaphoreType.DMA((count // lanes, lanes - 1)),
     ]
+
+
+def turn(vectors, cosine, sine_part, direction):
+    half = vectors.shape[-1] // 2
+    low, high = vectors[:, :half], vectors[:, half:]
+    return jnp.concatenate(
+        [
+            low * cosine - direction * high * sine_part,
+            high * cosine + direction * low * sine_part,
+        ],
+        -1,
+    )
+
+
+def product(left, right, left_dim, right_dim):
+    return lax.dot_general(
+        left, right, (((left_dim,), (right_dim,)), ((), ())), preferred_element_type=jnp.float32
+    )
+
+
+def attend_kernel(
+    width_q,
+    proj_ref,
+    cos_ref,
+    sin_ref,
+    cot_ref,
+    block_ref,
+    out_ref,
+    blocks_ref,
+    held,
+    before,
+    back_out,
+    back_in,
+    own_grad,
+    own_sem,
+    kv_sems,
+    back_sems,
+    *exchange_sems,
+):
+    rows = proj_ref.shape[0]
+    width_k = (proj_ref.shape[1] - width_q) // 2
+    heads_k = width_k // HD
+    group = width_q // width_k
+    inv_scale = 1.0 / math.sqrt(HD)
+    seqs, seq, dp = lax.axis_size("seq"), lax.axis_index("seq"), lax.axis_index("dp")
+    own = pltpu.make_async_copy(block_ref.at[seq, dp], blocks_ref.at[dp, seq], own_sem)
+    own.start()
+    cosine, sine_part = cos_ref[...], sin_ref[...]
+    for head in range(heads_k):
+        low = head * HD
+        at = slice(low, low + HD)
+        keys = proj_ref[:, width_q + low : width_q + low + HD]
+        held[:, at] = turn(keys, cosine, sine_part, 1.0).astype(jnp.bfloat16)
+        values = proj_ref[:, width_q + width_k + low : width_q + width_k + low + HD]
+        held[:, width_k + low : width_k + low + HD] = values.astype(jnp.bfloat16)
+    _, peers = block_peers()
+    greet(
+        (),
+        [{"seq": other, "dp": far} for _, other, far in peers]
+        + [{"tensor": other} for other in tensor_peers()],
+    )
+    ahead = pltpu.make_async_remote_copy(
+        src_ref=held,
+        dst_ref=before,
+        send_sem=kv_sems.at[0],
+        recv_sem=kv_sems.at[1],
+        device_id={"seq": seq + 1},
+        device_id_type=MESH,
+    )
+    behind = pltpu.make_async_remote_copy(
+        src_ref=back_out,
+        dst_ref=back_in,
+        send_sem=back_sems.at[0],
+        recv_sem=back_sems.at[1],
+        device_id={"seq": seq - 1},
+        device_id_type=MESH,
+    )
+    has_next, has_last = seq < seqs - 1, seq > 0
+
+    @pl.when(has_next)
+    def _():
+        ahead.start()
+
+    exchange = Exchange(block_ref, blocks_ref, *exchange_sems)
+    walk = exchange.steps()
+    next(walk)
+
+    queries = []
+    for head in range(heads_k * group):
+        part = proj_ref[:, head * HD : (head + 1) * HD]
+        queries.append(turn(part, cosine, sine_part, 1.0).astype(jnp.bfloat16))
+
+    @pl.when(has_last)
+    def _():
+        ahead.wait_recv()
+
+    @pl.when(jnp.logical_not(has_last))
+    def _():
+        before[...] = jnp.zeros_like(before)
+
+    query_at = lax.broadcasted_iota(jnp.int32, (rows, rows), 0)
+    key_at = lax.broadcasted_iota(jnp.int32, (rows, rows), 1)
+    masks = (
+        (key_at > query_at + (rows - WINDOW)) & (seq * rows - rows + key_at >= 0),
+        (key_at <= query_at) & (key_at > query_at - WINDOW),
+    )
+    for head in range(heads_k):
+        at = slice(head * HD, (head + 1) * HD)
+        at_value = slice(width_k + head * HD, width_k + (head + 1) * HD)
+        sides = (before, held)
+        key_grads, value_grads = [0.0, 0.0], [0.0, 0.0]
+        for member in range(group):
+            index = head * group + member
+            query = queries[index]
+            cot = cot_ref[:, index * HD : (index + 1) * HD]
+            squashes, terms, slopes = [], [], []
+            for side, mask in zip(sides, masks):
+                squash = jnp.tanh(product(query, side[:, at], 1, 1) * inv_scale / SOFTCAP)
+                squashes.append(squash)
+                terms.append(jnp.where(mask, jnp.exp(SOFTCAP * squash), 0.0))
+                slopes.append(product(cot, side[:, at_value], 1, 1))
+            total = sum(jnp.sum(term, -1, keepdims=True) for term in terms)
+            probs = [term / total for term in terms]
+            delta = sum(
+                jnp.sum(prob * slope, -1, keepdims=True) for prob, slope in zip(probs, slopes)
+            )
+            dquery = 0.0
+            for which in range(2):
+                prob, squash = probs[which], squashes[which]
+                dlogits = (
+                    prob * (slopes[which] - delta) * (1.0 - squash * squash) * inv_scale
+                ).astype(jnp.bfloat16)
+                dquery = dquery + product(dlogits, sides[which][:, at], 1, 0)
+                key_grads[which] = key_grads[which] + product(dlogits, query, 0, 0)
+                value_grads[which] = value_grads[which] + product(
+                    prob.astype(jnp.bfloat16), cot, 0, 0
+                )
+            out_ref[:, index * HD : (index + 1) * HD] = turn(
+                dquery, cosine, sine_part, -1.0
+            ).astype(jnp.bfloat16)
+        back_out[:, at] = key_grads[0].astype(jnp.bfloat16)
+        back_out[:, at_value] = value_grads[0].astype(jnp.bfloat16)
+        own_grad[:, at] = key_grads[1]
+        own_grad[:, at_value] = value_grads[1]
+
+    @pl.when(has_last)
+    def _():
+        behind.start()
+
+    next(walk)
+
+    @pl.when(has_next)
+    def _():
+        behind.wait_recv()
+        own_grad[...] += back_in[...].astype(jnp.float32)
+
+    for head in range(heads_k):
+        at = slice(head * HD, (head + 1) * HD)
+        out_ref[:, width_q + head * HD : width_q + (head + 1) * HD] = turn(
+            own_grad[:, at], cosine, sine_part, -1.0
+        ).astype(jnp.bfloat16)
+    out_ref[:, width_q + width_k :] = own_grad[:, width_k:].astype(jnp.bfloat16)
+
+    @pl.when(has_next)
+    def _():
+        ahead.wait_send()
+
+    @pl.when(has_last)
+    def _():
+        behind.wait_send()
+
+    exchange.finish()
+    own.wait()
+
+
+def attend_and_exchange(projected, cosine, sine_part, cotangent, blocks, collective_id):
+    rows, width_q = cotangent.shape
+    width_k = (projected.shape[1] - width_q) // 2
+    return pl.pallas_call(
+        functools.partial(attend_kernel, width_q),
+        out_shape=(
+            jax.ShapeDtypeStruct(projected.shape, jnp.bfloat16),
+            jax.ShapeDtypeStruct(
+                (blocks.shape[1], blocks.shape[0]) + blocks.shape[2:], blocks.dtype
+            ),
+        ),
+        in_specs=[pl.BlockSpec(memory_space=pltpu.VMEM)] * 5,
+        out_specs=(pl.BlockSpec(memory_space=pltpu.VMEM), pl.BlockSpec(memory_space=pl.ANY)),
+        scratch_shapes=[
+            pltpu.VMEM((rows, 2 * width_k), jnp.bfloat16),
+            pltpu.VMEM((rows, 2 * width_k), jnp.bfloat16),
+            pltpu.VMEM((rows, 2 * width_k), jnp.bfloat16),
+            pltpu.VMEM((rows, 2 * width_k), jnp.bfloat16),
+            pltpu.VMEM((rows, 2 * width_k), jnp.float32),
+            pltpu.SemaphoreType.DMA,
+            pltpu.SemaphoreType.DMA((2,)),
+            pltpu.SemaphoreType.DMA((2,)),
+        ]
+        + exchange_semaphores(),
+        compiler_params=pltpu.CompilerParams(
+            collective_id=collective_id, has_side_effects=True
+        ),
+    )(projected, cosine, sine_part, cotangent, blocks)
 
 
 def total_kernel(x_ref, out_ref, held, send_sem, recv_sem, send_wide, recv_wide, own_sem):
@@ -531,53 +663,19 @@
     local_w = jnp.concatenate([w_query, w_key, w_value], 1)
     seqs, dps = lax.axis_size("seq"), lax.axis_size("dp")
     rows_w = local_w.shape[0]
-    full_w, slabs = gather_and_exchange(
-        local_w, normed.T.reshape(seqs, dps, rows_w, row_count), cut_of(rows_w), 0
-    )
+    full_w = gather_blocks(local_w, cut_of(rows_w), ("seq", "dp"), 0)
     full_w = full_w.reshape(seqs * dps * rows_w, -1)
     projected = jnp.dot(normed, full_w, preferred_element_type=jnp.float32)
     start_row = lax.axis_index("seq") * row_count
-    query_pos = start_row + jnp.arange(row_count, dtype=jnp.int32)
-    key_pos = start_row - row_count + jnp.arange(2 * row_count, dtype=jnp.int32)
-    cosine, sine_part = angles(query_pos, HD)
-    heads_q = width_q // HD
-    heads_k = width_k // HD
-    rotated_query = rotate(
-        projected[:, :width_q].reshape(row_count, heads_q, HD), cosine, sine_part, 1.0
-    ).astype(jnp.bfloat16)
-    rotated_keys = rotate(
-        projected[:, width_q : width_q + width_k].reshape(row_count, heads_k, HD),
-        cosine,
-        sine_part,
-        1.0,
-    ).astype(jnp.bfloat16)
-    value_rows = (
-        projected[:, width_q + width_k :].reshape(row_count, heads_k, HD).astype(jnp.bfloat16)
-    )
-    keys_before, values_before = shifted((rotated_keys, value_rows), "seq", 1)
-    dquery, key_ext_grad, value_ext_grad = attend(
-        rotated_query,
-        jnp.concatenate([keys_before, rotated_keys], 0),
-        jnp.concatenate([values_before, value_rows], 0),
-        query_pos,
-        key_pos,
+    cosine, sine_part = angles(start_row + jnp.arange(row_count, dtype=jnp.int32), HD)
+    d_out, slabs = attend_and_exchange(
+        projected,
+        cosine[:, 0],
+        sine_part[:, 0],
         attn_grad[0],
-    )
-    back_keys, back_values = shifted(
-        (key_ext_grad[:row_count], value_ext_grad[:row_count]), "seq", -1
-    )
-    key_grads = key_ext_grad[row_count:] + back_keys
-    value_grads = value_ext_grad[row_count:] + back_values
-    dquery = rotate(dquery, cosine, sine_part, -1.0)
-    key_grads = rotate(key_grads, cosine, sine_part, -1.0)
-    d_out = jnp.concatenate(
-        [
-            dquery.reshape(row_count, width_q),
-            key_grads.reshape(row_count, width_k),
-            value_grads.reshape(row_count, width_k),
-        ],
-        1,
-    ).astype(jnp.bfloat16)
+        normed.T.reshape(seqs, dps, rows_w, row_count),
+        3,
+    )
     dnormed = lax.dot_general(
         d_out, full_w, (((1,), (1,)), ((), ())), preferred_element_type=jnp.float32
     )

time: 245 us -> 242 us (0.988)
  Pallas kernels: 158 us -> 190 us
  waiting for transfers between devices: 10.4 us -> 0 us
  starting transfers between devices: 10 us -> 0 us
  other arithmetic: 26.7 us -> 18.6 us
  matrix products: 26.6 us -> 23.5 us
  local copies, waits for them, and re-layouts: 11.4 us -> 8.72 us
    pallas_call x1 -> x2, Pallas kernels: 89.7 us -> 120 us  [the longest x1 86.9 us: gather_blocks(): pl.pallas_call(functools.partial(gather_kernel, cut, order), out_shape=ja...]
    ppermute x4 -> x0, waiting for transfers between devices: 10.4 us -> none  [shifted(): lax.ppermute(value, axis, [(source, source + steps) for source in range(l...]
    ppermute x4 -> x0, starting transfers between devices: 10 us -> none  [shifted(): lax.ppermute(value, axis, [(source, source + steps) for source in range(l...]
    dot_general x5 -> x0, matrix products: 4.97 us -> none  [the longest x1 1.48 us: attend(): jnp.einsum('tkgd,skd->kgts', grouped_query, key_rows, preferred_element_t...]
    dot_general x1, matrix products: 4.06 us -> 7.26 us  [local(): lax.dot_general(d_out, full_w, (((1,), (1,)), ((), ())), preferred_elemen...]
  transfers between devices with their start and end apart: 4 -> 0, of which waited for: 2 -> 0; matrix products, arithmetic and copies ran while one was open for 4% -> 0% of each run, Pallas kernels for 0% -> 0%
where the time goes in v4:
time: 242 us
  Pallas kernels  190 us (79%)
  matrix products  23.5 us (10%)
  other arithmetic  18.6 us (8%)
  local copies, waits for them, and re-layouts  8.72 us (4%)
    pallas_call x1, Pallas kernels, gather_blocks(): pl.pallas_call(functools.partial(gather_kernel, cut, order), out_shape=ja...  86.9 us
    pallas_call x1, Pallas kernels, gather_and_scatter(): pl.pallas_call(functools.partial(tail_kernel, cut, order), out_shape=(jax...  58.2 us
    pallas_call x1, Pallas kernels, attend_and_exchange(): pl.pallas_call(functools.partial(attend_kernel, width_q), out_shape=(jax....  32.9 us
    pallas_call x1, Pallas kernels, total_of(): pl.pallas_call(total_kernel, out_shape=jax.ShapeDtypeStruct(x.shape, x.dt...  12 us
    dot_general x8, matrix products, local(): jnp.dot(slabs[example, s], cotangents[example, s], preferred_element_type...  10.1 us
    dot_general x1, matrix products, local(): lax.dot_general(d_out, full_w, (((1,), (1,)), ((), ())), preferred_elemen...  7.26 us
    dot_general x1, matrix products, local(): projected = jnp.dot(normed, full_w, preferred_element_type=jnp.float32)  6.16 us
    add x1, other arithmetic, local(): clipped = sum((factor[example] * grads[example] for example in range(dps)))  5.95 us

profile of v4, /device:TPU:0, one launch (start us, length us, event | category | flops | bytes accessed | tf_op | source)
XLA Modules:
  0.0 241.6 jit_solution(5227486092366576992)
XLA Ops:
  0.6 0.0 copy-start.3
  0.6 0.0 copy-start.5
  0.7 0.0 copy-start.4
  0.7 2.0 fusion
  2.7 0.0 copy-done.3
  2.7 0.0 copy-done.5
  2.7 0.0 copy-done.4
  2.7 1.0 pad_maximum_fusion.x_ref
  3.8 0.0 copy-start
  3.8 0.0 copy-start.6
  3.8 86.9 %shard_map.93 = bf16[2,4,448,1024]{3,2,1,0:T(8,128)(2,1)} custom-call(bf16[448,1024]{1,0:T(8,128)(2,1)} %pad_maximum_fusion.x_ref), custom_call_target="tpu_custom_call" | custom-call | tf_op jit(solution)/shard_map/pallas_call | solution.py:165
  90.6 0.0 copy-done
  90.6 0.0 copy-done.6
  90.6 6.2 %fusion.6.proj_ref = f32[256,1024]{1,0:T(8,128)} fusion(bf16[3584,1024]{1,0:T(8,128)(2,1)} %bitcast.115, bf16[1,256,3584]{2,1,0:T(8,128)(2,1)S(1)} %copy-done, f32[3584]{0:T(1024)S(1)} %copy-done.6, f32[256]{0:T(256)S(1)} %get-tuple-element.25), kind=kOutput, calls=%fused_computation.11 | convolution fusion | flops 1882718208 | bytes 10238976 | tf_op jit(solution)/shard_map/dot_general | solution.py:668
  96.8 1.8 fusion.8
  98.6 3.8 %copy.10 = bf16[3584,256]{1,0:T(8,128)(2,1)} copy(bf16[3584,256]{0,1:T(8,128)(2,1)} %fusion.8) | data formatting | bytes 3670016 | tf_op jit(solution)/shard_map/transpose | solution.py:676
  102.5 1.2 multiply_sine_fusion
  103.7 32.9 %shard_map.94 = (bf16[256,1024]{1,0:T(8,128)(2,1)}, bf16[4,2,448,256]{3,2,1,0:T(8,128)(2,1)}) custom-call(f32[256,1024]{1,0:T(8,128)} %fusion.6.proj_ref, f32[256,128]{1,0:T(8,128)} %get-tuple-element.23.cos_ref, f32[256,128]{1,0:T(8,128)} %get-tuple-element.22.sin_ref, bf16[256,512]{1,0:T(8,128)(2,1)} %bitcast.117, bf16[2,4,448,256]{3,2,1,0:T(8,128)(2,1)} %bitcast.114), custom_call_target="tpu_custom_call" | custom-call | tf_op jit(solution)/shard_map/pallas_call | solution.py:551
  136.6 7.3 %fusion.4 = (f32[256]{0:T(256)}, bf16[256,3584]{1,0:T(8,128)(2,1)}) fusion(bf16[1,256,3584]{2,1,0:T(8,128)(2,1)S(1)} %copy-done, f32[3584]{0:T(1024)S(1)} %copy-done.6, bf16[256,1024]{1,0:T(8,128)(2,1)} %get-tuple-element.10.x_ref, bf16[3584,1024]{1,0:T(8,128)(2,1)} %bitcast.116), kind=kOutput, calls=%fused_computation.7 | convolution fusion | flops 1883635456 | bytes 11549696 | tf_op jit(solution)/shard_map/dot_general | solution.py:679
  143.8 58.2 %shard_map.95 = (bf16[4,2,256,1024]{3,2,1,0:T(8,128)(2,1)}, bf16[4,256,896]{2,1,0:T(8,128)(2,1)}, f32[4,2,128]{2,1,0:T(2,128)}) custom-call(bf16[256,1024]{1,0:T(8,128)(2,1)} %get-tuple-element.10.x_ref, bf16[256,3584]{1,0:T(8,128)(2,1)} %get-tuple-element.15.part_ref, f32[2,128]{1,0:T(2,128)} %bitcast.118), custom_call_target="tpu_custom_call" | custom-call | tf_op jit(solution)/shard_map/pallas_call | solution.py:257
  202.1 0.0 copy-start.7
  202.1 1.8 convert_reduce_fusion
  203.9 0.0 copy-done.7
  204.0 0.1 dynamic_slice.8
  204.1 0.0 copy-start.1
  204.1 0.4 convert_element_type.38
  204.5 0.0 copy-start.2
  204.5 1.0 fusion.34
  205.5 0.9 copy-done.1
  206.4 0.7 copy-done.2
  207.1 0.4 fusion.24
  207.5 1.2 multiply_reduce_fusion.3
  208.7 0.4 fusion.21
  209.1 2.4 %multiply_reduce_fusion.2 = (f32[]{:T(128)}, f32[448,1024]{1,0:T(8,128)}) fusion(f32[448,1024]{1,0:T(8,128)S(1)} %fusion.21, bf16[4,2,256,1024]{3,2,1,0:T(8,128)(2,1)S(1)} %copy-done.1, bf16[4,2,448,256]{3,2,1,0:T(8,128)(2,1)S(1)} %copy-done.2), kind=kOutput, calls=%fused_computation.16 | convolution fusion | flops 236257280 | bytes 4423684 | tf_op jit(solution)/shard_map/dot_general | solution.py:690
  211.6 0.4 fusion.18
  212.0 2.4 multiply_reduce_fusion.1
  214.4 0.4 fusion.15
  214.8 2.4 %multiply_reduce_fusion = (f32[]{:T(128)}, f32[448,1024]{1,0:T(8,128)}) fusion(f32[448,1024]{1,0:T(8,128)S(1)} %fusion.15, bf16[4,2,256,1024]{3,2,1,0:T(8,128)(2,1)S(1)} %copy-done.1, bf16[4,2,448,256]{3,2,1,0:T(8,128)(2,1)S(1)} %copy-done.2), kind=kOutput, calls=%fused_computation.14 | convolution fusion | flops 236257280 | bytes 4423684 | tf_op jit(solution)/shard_map/dot_general | solution.py:690
  217.2 2.6 %pad_maximum_fusion.1 = f32[4]{0:T(128)S(1)} fusion(f32[1]{0:T(128)} %bitcast.26, f32[1]{0:T(128)} %bitcast.21, f32[1]{0:T(128)} %bitcast.16, f32[1]{0:T(128)} %bitcast.11), kind=kLoop, calls=%fused_computation.73 | loop fusion | flops 12 | bytes 32 | tf_op jit(solution)/shard_map/stack | solution.py:696
  219.8 0.7 broadcast_in_dim.4.x_ref
  220.4 12.0 %shard_map.96 = f32[4,128]{1,0:T(4,128)} custom-call(f32[4,128]{1,0:T(4,128)} %broadcast_in_dim.4.x_ref), custom_call_target="tpu_custom_call" | custom-call | tf_op jit(solution)/shard_map/pallas_call | solution.py:633
  232.5 0.7 maximum_divide_fusion
  233.2 0.5 fusion.52
  233.7 5.9 %multiply_add_fusion = f32[448,1024]{1,0:T(8,128)S(1)} fusion(f32[448,1024]{1,0:T(8,128)} %get-tuple-element.28, f32[448,1024]{1,0:T(8,128)} %get-tuple-element.30, f32[448,1024]{1,0:T(8,128)} %get-tuple-element.32, f32[448,1024]{1,0:T(8,128)S(1)} %get-tuple-element.34, f32[]{:T(128)} %bitcast.30, f32[]{:T(128)} %bitcast.29, f32[]{:T(128)} %bitcast.28, ...), kind=kLoop, calls=%fused_computation.13 | loop fusion | flops 3211264 | bytes 9175056 | tf_op jit(solution)/shard_map/add | solution.py:700
  239.6 1.0 fusion.51
  240.6 1.0 slice.100
  (5 shorter events, 0.0 us)
Async XLA Ops:
  0.6 2.1 copy-start.3
  0.6 2.1 copy-start.5
  0.7 2.1 copy-start.4
  3.8 86.9 %copy-start = (bf16[1,256,3584]{2,1,0:T(8,128)(2,1)S(1)}, bf16[1,256,3584]{2,1,0:T(8,128)(2,1)}, u32[]{:S(2)}) copy-start(bf16[1,256,3584]{2,1,0:T(8,128)(2,1)} %param.6) | copy-start | bytes 5505028
  3.8 86.9 %copy-start.6 = (f32[3584]{0:T(1024)S(1)}, f32[3584]{0:T(1024)}, u32[]{:S(2)}) copy-start(f32[3584]{0:T(1024)} %param.10) | copy-start | bytes 43012
  202.1 1.9 copy-start.7
  204.1 2.4 copy-start.1
  204.5 2.6 %copy-start.2 = (bf16[4,2,448,256]{3,2,1,0:T(8,128)(2,1)S(1)}, bf16[4,2,448,256]{3,2,1,0:T(8,128)(2,1)}, u32[]{:S(2)}) copy-start(bf16[4,2,448,256]{3,2,1,0:T(8,128)(2,1)} %get-tuple-element.9) | copy-start | bytes 5505028

commit v5 on v4

--- a/solution.py
+++ b/solution.py
@@ -186,9 +186,11 @@
     x_ref,
     part_ref,
     inner_ref,
+    block_ref,
     out_ref,
     parts_ref,
     inners_ref,
+    blocks_ref,
     send_sem,
     recv_sem,
     own_sem,
@@ -196,6 +198,8 @@
     part_recv,
     inner_send,
     inner_recv,
+    block_send,
+    block_recv,
 ):
     rows = x_ref.shape[0]
     count, me = lax.axis_size("tensor"), lax.axis_index("tensor")
@@ -210,6 +214,7 @@
         ),
         pltpu.make_async_copy(slab(me), parts_ref.at[me], own_sem.at[1]),
         pltpu.make_async_copy(inner_ref, inners_ref.at[me], own_sem.at[2]),
+        pltpu.make_async_copy(block_ref, blocks_ref.at[me], own_sem.at[3]),
     ]
     for own in owns:
         own.start()
@@ -237,6 +242,17 @@
                 device_id_type=MESH,
             )
         )
+    for index, other in enumerate(others):
+        copies.append(
+            pltpu.make_async_remote_copy(
+                src_ref=block_ref,
+                dst_ref=blocks_ref.at[me],
+                send_sem=block_send.at[index],
+                recv_sem=block_recv.at[index],
+                device_id={"tensor": other},
+                device_id_type=MESH,
+            )
+        )
     for copy in copies:
         copy.start()
     run_gathers(
@@ -251,7 +267,7 @@
         own.wait()
 
 
-def gather_and_scatter(x, part, inner, cut, order, collective_id):
+def gather_and_scatter(x, part, inner, block, cut, order, collective_id):
     shape = (lax.axis_size("seq"), lax.axis_size("dp"))
     count = lax.axis_size("tensor")
     return pl.pallas_call(
@@ -260,19 +276,20 @@
             jax.ShapeDtypeStruct(tuple(lax.axis_size(axis) for axis in order) + x.shape, x.dtype),
             jax.ShapeDtypeStruct((count, part.shape[0], part.shape[1] // count), part.dtype),
             jax.ShapeDtypeStruct((count,) + inner.shape, inner.dtype),
-        ),
-        in_specs=[pl.BlockSpec(memory_space=pltpu.VMEM)] * 3,
-        out_specs=(pl.BlockSpec(memory_space=pl.ANY),) * 3,
+            jax.ShapeDtypeStruct((count,) + block.shape, block.dtype),
+        ),
+        in_specs=[pl.BlockSpec(memory_space=pltpu.VMEM)] * 4,
+        out_specs=(pl.BlockSpec(memory_space=pl.ANY),) * 4,
         scratch_shapes=[
             pltpu.SemaphoreType.DMA((2, 4) + shape),
             pltpu.SemaphoreType.DMA((2,) + shape),
-            pltpu.SemaphoreType.DMA((3,)),
+            pltpu.SemaphoreType.DMA((4,)),
         ]
-        + [pltpu.SemaphoreType.DMA((count - 1,))] * 4,
+        + [pltpu.SemaphoreType.DMA((count - 1,))] * 6,
         compiler_params=pltpu.CompilerParams(
             collective_id=collective_id, has_side_effects=True
         ),
-    )(x, part, inner)
+    )(x, part, inner, block)
 
 
 def block_peers():
@@ -288,87 +305,58 @@
 
 
 class Exchange:
-    def __init__(self, x_ref, out_ref, send_sem, recv_sem, pass_sem):
+    def __init__(self, x_ref, out_ref, send_sem, recv_sem, own_sem):
         self.x_ref, self.out_ref = x_ref, out_ref
-        self.send_sem, self.recv_sem, self.pass_sem = send_sem, recv_sem, pass_sem
-        self.seqs, self.dps = lax.axis_size("seq"), lax.axis_size("dp")
+        self.send_sem, self.recv_sem, self.own_sem = send_sem, recv_sem, own_sem
         self.lanes, self.lane = lax.axis_size("tensor"), lax.axis_index("tensor")
         self.mine, self.peers = block_peers()
         self.sender = lax.rem(self.mine, self.lanes) == self.lane
 
-    def slot(self, index):
-        return self.out_ref.at[index // self.seqs, lax.rem(index, self.seqs)]
-
-    def first(self, hop):
+    def copy(self, hop, slot):
         _, seq, dp = self.peers[hop]
         return pltpu.make_async_remote_copy(
             src_ref=self.x_ref.at[seq, dp],
-            dst_ref=self.slot(self.mine),
+            dst_ref=self.out_ref.at[slot],
             send_sem=self.send_sem.at[hop],
-            recv_sem=self.recv_sem.at[self.mine],
+            recv_sem=self.recv_sem.at[slot],
             device_id={"seq": seq, "dp": dp},
             device_id_type=MESH,
         )
 
-    def onward(self, index, step, hop, other):
-        return pltpu.make_async_remote_copy(
-            src_ref=self.slot(index),
-            dst_ref=self.slot(index),
-            send_sem=self.pass_sem.at[step, hop],
-            recv_sem=self.recv_sem.at[index],
-            device_id={"tensor": other},
-            device_id_type=MESH,
-        )
-
-    def owned(self, lane):
-        return [lane + step * self.lanes for step in range(self.seqs * self.dps // self.lanes)]
-
-    def steps(self):
+    def own(self):
+        return pltpu.make_async_copy(
+            self.x_ref.at[lax.axis_index("seq"), lax.axis_index("dp")],
+            self.out_ref.at[self.mine // self.lanes],
+            self.own_sem,
+        )
+
+    def start(self):
         @pl.when(self.sender)
         def _():
             for hop in range(len(self.peers)):
-                self.first(hop).start()
-
-        yield
-        others = tensor_peers()
-        for step, index in enumerate(self.owned(self.lane)):
-
-            @pl.when(index != self.mine)
+                self.copy(hop, self.mine // self.lanes).start()
+            self.own().start()
+
+    def finish(self):
+        for slot in range((len(self.peers) + 1) // self.lanes):
+
+            @pl.when(self.lane + slot * self.lanes != self.mine)
             def _():
-                self.onward(index, step, 0, others[0]).wait_recv()
-                for hop, other in enumerate(others):
-                    self.onward(index, step, hop, other).start()
-
-        yield
-
-    def finish(self):
-        others = tensor_peers()
-        for other in others:
-            for index in self.owned(other):
-
-                @pl.when(index != self.mine)
-                def _():
-                    self.onward(index, 0, 0, other).wait_recv()
-
-        for step, index in enumerate(self.owned(self.lane)):
-
-            @pl.when(index != self.mine)
-            def _():
-                for hop, other in enumerate(others):
-                    self.onward(index, step, hop, other).wait_send()
+                self.copy(0, slot).wait_recv()
 
         @pl.when(self.sender)
         def _():
             for hop in range(len(self.peers)):
-                self.first(hop).wait_send()
+                self.copy(hop, self.mine // self.lanes).wait_send()
+            self.own().wait()
 
 
 def exchange_semaphores():
     count, lanes = lax.axis_size("seq") * lax.axis_size("dp"), lax.axis_size("tensor")
     return [
         pltpu.SemaphoreType.DMA((count - 1,)),
-        pltpu.SemaphoreType.DMA((count,)),
-        pltpu.SemaphoreType.DMA((count // lanes, lanes - 1)),
+        pltpu.SemaphoreType.DMA((count // lanes,)),
+        pltpu.SemaphoreType.DMA,
     ]
 
 
@@ -404,7 +392,6 @@
     back_out,
     back_in,
     own_grad,
-    own_sem,
     kv_sems,
     back_sems,
     *exchange_sems,
@@ -414,9 +401,7 @@
     heads_k = width_k // HD
     group = width_q // width_k
     inv_scale = 1.0 / math.sqrt(HD)
-    seqs, seq, dp = lax.axis_size("seq"), lax.axis_index("seq"), lax.axis_index("dp")
-    own = pltpu.make_async_copy(block_ref.at[seq, dp], blocks_ref.at[dp, seq], own_sem)
-    own.start()
+    seqs, seq = lax.axis_size("seq"), lax.axis_index("seq")
     cosine, sine_part = cos_ref[...], sin_ref[...]
     for head in range(heads_k):
         low = head * HD
@@ -426,11 +411,7 @@
         values = proj_ref[:, width_q + width_k + low : width_q + width_k + low + HD]
         held[:, width_k + low : width_k + low + HD] = values.astype(jnp.bfloat16)
     _, peers = block_peers()
-    greet(
-        (),
-        [{"seq": other, "dp": far} for _, other, far in peers]
-        + [{"tensor": other} for other in tensor_peers()],
-    )
+    greet((), [{"seq": other, "dp": far} for _, other, far in peers])
     ahead = pltpu.make_async_remote_copy(
         src_ref=held,
         dst_ref=before,
@@ -454,8 +435,7 @@
         ahead.start()
 
     exchange = Exchange(block_ref, blocks_ref, *exchange_sems)
-    walk = exchange.steps()
-    next(walk)
+    exchange.start()
 
     queries = []
     for head in range(heads_k * group):
@@ -519,8 +499,6 @@
     def _():
         behind.start()
 
-    next(walk)
-
     @pl.when(has_next)
     def _():
         behind.wait_recv()
@@ -542,7 +520,6 @@
         behind.wait_send()
 
     exchange.finish()
-    own.wait()
 
 
 def attend_and_exchange(projected, cosine, sine_part, cotangent, blocks, collective_id):
@@ -553,7 +530,9 @@
         out_shape=(
             jax.ShapeDtypeStruct(projected.shape, jnp.bfloat16),
             jax.ShapeDtypeStruct(
-                (blocks.shape[1], blocks.shape[0]) + blocks.shape[2:], blocks.dtype
+                (blocks.shape[0] * blocks.shape[1] // lax.axis_size("tensor"),)
+                + blocks.shape[2:],
+                blocks.dtype,
             ),
         ),
         in_specs=[pl.BlockSpec(memory_space=pltpu.VMEM)] * 5,
@@ -564,7 +543,6 @@
             pltpu.VMEM((rows, 2 * width_k), jnp.bfloat16),
             pltpu.VMEM((rows, 2 * width_k), jnp.bfloat16),
             pltpu.VMEM((rows, 2 * width_k), jnp.float32),
-            pltpu.SemaphoreType.DMA,
             pltpu.SemaphoreType.DMA((2,)),
             pltpu.SemaphoreType.DMA((2,)),
         ]
@@ -668,7 +646,7 @@
     projected = jnp.dot(normed, full_w, preferred_element_type=jnp.float32)
     start_row = lax.axis_index("seq") * row_count
     cosine, sine_part = angles(start_row + jnp.arange(row_count, dtype=jnp.int32), HD)
-    d_out, slabs = attend_and_exchange(
+    d_out, passed = attend_and_exchange(
         projected,
         cosine[:, 0],
         sine_part[:, 0],
@@ -680,15 +658,18 @@
         d_out, full_w, (((1,), (1,)), ((), ())), preferred_element_type=jnp.float32
     )
     inner = jnp.sum(widened * norm_gain[None, :] * dnormed, -1).reshape(-1, 128)
-    cotangents, parts, inners = gather_and_scatter(
-        d_out, dnormed.astype(jnp.bfloat16), inner, cut_of(row_count), ("dp", "seq"), 2
+    cotangents, parts, inners, slabs = gather_and_scatter(
+        d_out, dnormed.astype(jnp.bfloat16), inner, passed, cut_of(row_count), ("dp", "seq"), 2
     )
     grads = []
+    lanes = lax.axis_size("tensor")
     for example in range(dps):
         grads.append(
             sum(
                 jnp.dot(
-                    slabs[example, s], cotangents[example, s], preferred_element_type=jnp.float32
+                    slabs[(example * seqs + s) % lanes, (example * seqs + s) // lanes],
+                    cotangents[example, s],
+                    preferred_element_type=jnp.float32
                 )
                 for s in range(seqs)
             )

time: 242 us -> 224 us (0.926)
  Pallas kernels: 190 us -> 172 us
    pallas_call x1, Pallas kernels: 32.9 us -> 21.9 us  [attend_and_exchange(): pl.pallas_call(functools.partial(attend_kernel, width_q), out_shape=(jax....]
    pallas_call x1, Pallas kernels: 58.2 us -> 51.7 us  [gather_and_scatter(): pl.pallas_call(functools.partial(tail_kernel, cut, order), out_shape=(jax...]
where the time goes in v5:
time: 224 us; the launch traced here: 223 us
  Pallas kernels  172 us (77%)
  matrix products  23.6 us (11%)
  other arithmetic  18.6 us (8%)
  local copies, waits for them, and re-layouts  8.73 us (4%)
    pallas_call x1, Pallas kernels, gather_blocks(): pl.pallas_call(functools.partial(gather_kernel, cut, order), out_shape=ja...  86.9 us
    pallas_call x1, Pallas kernels, gather_and_scatter(): pl.pallas_call(functools.partial(tail_kernel, cut, order), out_shape=(jax...  51.7 us
    pallas_call x1, Pallas kernels, attend_and_exchange(): pl.pallas_call(functools.partial(attend_kernel, width_q), out_shape=(jax....  21.9 us
    pallas_call x1, Pallas kernels, total_of(): pl.pallas_call(total_kernel, out_shape=jax.ShapeDtypeStruct(x.shape, x.dt...  11.1 us
    dot_general x8, matrix products, local(): jnp.dot(slabs[(example * seqs + s) % lanes, (example * seqs + s) // lanes...  10.1 us
    dot_general x1, matrix products, local(): lax.dot_general(d_out, full_w, (((1,), (1,)), ((), ())), preferred_elemen...  7.33 us
    dot_general x1, matrix products, local(): projected = jnp.dot(normed, full_w, preferred_element_type=jnp.float32)  6.16 us
    add x1, other arithmetic, local(): clipped = sum((factor[example] * grads[example] for example in range(dps)))  5.95 us

profile of v5, /device:TPU:0, one launch (start us, length us, event | category | flops | bytes accessed | tf_op | source)
XLA Modules:
  0.0 223.3 jit_solution(15125711788191159381)
XLA Ops:
  0.6 0.0 copy-start.3
  0.6 0.0 copy-start.5
  0.7 0.0 copy-start.4
  0.7 2.0 fusion
  2.7 0.0 copy-done.3
  2.7 0.0 copy-done.5
  2.7 0.0 copy-done.4
  2.7 1.0 pad_maximum_fusion.x_ref
  3.8 0.0 copy-start
  3.8 0.0 copy-start.6
  3.8 86.9 %shard_map.93 = bf16[2,4,448,1024]{3,2,1,0:T(8,128)(2,1)} custom-call(bf16[448,1024]{1,0:T(8,128)(2,1)} %pad_maximum_fusion.x_ref), custom_call_target="tpu_custom_call" | custom-call | tf_op jit(solution)/shard_map/pallas_call | solution.py:165
  90.6 0.0 copy-done
  90.6 0.0 copy-done.6
  90.6 6.2 %fusion.6.proj_ref = f32[256,1024]{1,0:T(8,128)} fusion(bf16[3584,1024]{1,0:T(8,128)(2,1)} %bitcast.115, bf16[1,256,3584]{2,1,0:T(8,128)(2,1)S(1)} %copy-done, f32[3584]{0:T(1024)S(1)} %copy-done.6, f32[256]{0:T(256)S(1)} %get-tuple-element.27), kind=kOutput, calls=%fused_computation.11 | convolution fusion | flops 1882718208 | bytes 10238976 | tf_op jit(solution)/shard_map/dot_general | solution.py:646
  96.8 1.8 fusion.8
  98.6 3.8 %copy.10 = bf16[3584,256]{1,0:T(8,128)(2,1)} copy(bf16[3584,256]{0,1:T(8,128)(2,1)} %fusion.8) | data formatting | bytes 3670016 | tf_op jit(solution)/shard_map/transpose | solution.py:654
  102.4 1.2 multiply_sine_fusion
  103.7 21.9 %shard_map.94 = (bf16[256,1024]{1,0:T(8,128)(2,1)}, bf16[2,448,256]{2,1,0:T(8,128)(2,1)}) custom-call(f32[256,1024]{1,0:T(8,128)} %fusion.6.proj_ref, f32[256,128]{1,0:T(8,128)} %get-tuple-element.25.cos_ref, f32[256,128]{1,0:T(8,128)} %get-tuple-element.24.sin_ref, bf16[256,512]{1,0:T(8,128)(2,1)} %bitcast.117, bf16[2,4,448,256]{3,2,1,0:T(8,128)(2,1)} %bitcast.114), custom_call_target="tpu_custom_call" | custom-call | tf_op jit(solution)/shard_map/pallas_call | solution.py:528
  125.6 7.3 %fusion.4 = (f32[256]{0:T(256)}, bf16[256,3584]{1,0:T(8,128)(2,1)}) fusion(bf16[1,256,3584]{2,1,0:T(8,128)(2,1)S(1)} %copy-done, f32[3584]{0:T(1024)S(1)} %copy-done.6, bf16[256,1024]{1,0:T(8,128)(2,1)} %get-tuple-element.10.x_ref, bf16[3584,1024]{1,0:T(8,128)(2,1)} %bitcast.116), kind=kOutput, calls=%fused_computation.7 | convolution fusion | flops 1883635456 | bytes 11549696 | tf_op jit(solution)/shard_map/dot_general | solution.py:657
  132.9 51.7 %shard_map.95 = (bf16[4,2,256,1024]{3,2,1,0:T(8,128)(2,1)}, bf16[4,256,896]{2,1,0:T(8,128)(2,1)}, f32[4,2,128]{2,1,0:T(2,128)}, bf16[4,2,448,256]{3,2,1,0:T(8,128)(2,1)}) custom-call(bf16[256,1024]{1,0:T(8,128)(2,1)} %get-tuple-element.10.x_ref, bf16[256,3584]{1,0:T(8,128)(2,1)} %get-tuple-element.17.part_ref, f32[2,128]{1,0:T(2,128)} %bitcast.118, ...), custom_call_target="tpu_custom_call" | custom-call | tf_op jit(solution)/shard_map/pallas_call | solution.py:273
  184.7 0.0 copy-start.7
  184.7 1.8 convert_reduce_fusion
  186.5 0.0 copy-done.7
  186.6 0.1 dynamic_slice.8
  186.7 0.0 copy-start.1
  186.7 0.4 convert_element_type.38
  187.1 0.0 copy-start.2
  187.1 1.0 fusion.34
  188.1 0.9 copy-done.1
  189.0 0.7 copy-done.2
  189.7 0.4 fusion.24
  190.1 1.2 multiply_reduce_fusion.3
  191.3 0.4 fusion.21
  191.7 2.4 %multiply_reduce_fusion.2 = (f32[]{:T(128)}, f32[448,1024]{1,0:T(8,128)}) fusion(f32[448,1024]{1,0:T(8,128)S(1)} %fusion.21, bf16[4,2,256,1024]{3,2,1,0:T(8,128)(2,1)S(1)} %copy-done.1, bf16[4,2,448,256]{3,2,1,0:T(8,128)(2,1)S(1)} %copy-done.2), kind=kOutput, calls=%fused_computation.16 | convolution fusion | flops 236257280 | bytes 4423684 | tf_op jit(solution)/shard_map/dot_general | solution.py:669
  194.2 0.4 fusion.18
  194.6 2.4 %multiply_reduce_fusion.1 = (f32[]{:T(128)}, f32[448,1024]{1,0:T(8,128)}) fusion(f32[448,1024]{1,0:T(8,128)S(1)} %fusion.18, bf16[4,2,256,1024]{3,2,1,0:T(8,128)(2,1)S(1)} %copy-done.1, bf16[4,2,448,256]{3,2,1,0:T(8,128)(2,1)S(1)} %copy-done.2), kind=kOutput, calls=%fused_computation.15 | convolution fusion | flops 236257280 | bytes 4423684 | tf_op jit(solution)/shard_map/dot_general | solution.py:669
  197.0 0.4 fusion.15
  197.4 2.4 %multiply_reduce_fusion = (f32[]{:T(128)}, f32[448,1024]{1,0:T(8,128)}) fusion(f32[448,1024]{1,0:T(8,128)S(1)} %fusion.15, bf16[4,2,256,1024]{3,2,1,0:T(8,128)(2,1)S(1)} %copy-done.1, bf16[4,2,448,256]{3,2,1,0:T(8,128)(2,1)S(1)} %copy-done.2), kind=kOutput, calls=%fused_computation.14 | convolution fusion | flops 236257280 | bytes 4423684 | tf_op jit(solution)/shard_map/dot_general | solution.py:669
  199.8 2.6 %pad_maximum_fusion.1 = f32[4]{0:T(128)S(1)} fusion(f32[1]{0:T(128)} %bitcast.26, f32[1]{0:T(128)} %bitcast.21, f32[1]{0:T(128)} %bitcast.16, f32[1]{0:T(128)} %bitcast.11), kind=kLoop, calls=%fused_computation.73 | loop fusion | flops 12 | bytes 32 | tf_op jit(solution)/shard_map/stack | solution.py:677
  202.4 0.7 broadcast_in_dim.4.x_ref
  203.0 11.1 %shard_map.96 = f32[4,128]{1,0:T(4,128)} custom-call(f32[4,128]{1,0:T(4,128)} %broadcast_in_dim.4.x_ref), custom_call_target="tpu_custom_call" | custom-call | tf_op jit(solution)/shard_map/pallas_call | solution.py:611
  214.1 0.7 maximum_divide_fusion
  214.8 0.5 fusion.52
  215.4 5.9 %multiply_add_fusion = f32[448,1024]{1,0:T(8,128)S(1)} fusion(f32[448,1024]{1,0:T(8,128)} %get-tuple-element.30, f32[448,1024]{1,0:T(8,128)} %get-tuple-element.32, f32[448,1024]{1,0:T(8,128)} %get-tuple-element.34, f32[448,1024]{1,0:T(8,128)S(1)} %get-tuple-element.36, f32[]{:T(128)} %bitcast.30, f32[]{:T(128)} %bitcast.29, f32[]{:T(128)} %bitcast.28, ...), kind=kLoop, calls=%fused_computation.13 | loop fusion | flops 3211264 | bytes 9175056 | tf_op jit(solution)/shard_map/add | solution.py:681
  221.3 1.0 fusion.51
  222.3 1.0 slice.100
  (5 shorter events, 0.0 us)
Async XLA Ops:
  0.6 2.1 copy-start.3
  0.6 2.1 copy-start.5
  0.7 2.1 copy-start.4
  3.8 86.9 %copy-start = (bf16[1,256,3584]{2,1,0:T(8,128)(2,1)S(1)}, bf16[1,256,3584]{2,1,0:T(8,128)(2,1)}, u32[]{:S(2)}) copy-start(bf16[1,256,3584]{2,1,0:T(8,128)(2,1)} %param.6) | copy-start | bytes 5505028
  3.8 86.9 %copy-start.6 = (f32[3584]{0:T(1024)S(1)}, f32[3584]{0:T(1024)}, u32[]{:S(2)}) copy-start(f32[3584]{0:T(1024)} %param.10) | copy-start | bytes 43012
  184.7 1.9 copy-start.7
  186.7 2.4 %copy-start.1 = (bf16[4,2,256,1024]{3,2,1,0:T(8,128)(2,1)S(1)}, bf16[4,2,256,1024]{3,2,1,0:T(8,128)(2,1)}, u32[]{:S(2)}) copy-start(bf16[4,2,256,1024]{3,2,1,0:T(8,128)(2,1)} %get-tuple-element.13) | copy-start | bytes 12582916
  187.1 2.6 %copy-start.2 = (bf16[4,2,448,256]{3,2,1,0:T(8,128)(2,1)S(1)}, bf16[4,2,448,256]{3,2,1,0:T(8,128)(2,1)}, u32[]{:S(2)}) copy-start(bf16[4,2,448,256]{3,2,1,0:T(8,128)(2,1)} %get-tuple-element.12) | copy-start | bytes 5505028
